TPU v7x, 256 devices: a whole 4x4x8 slice. The times are simulated.
256 devices in a mesh: dp: 16 (over y, x), seq: 16 (over z, core).
Axes of the slice: x: 4, y: 4, z: 8, core: 2. Of those that a mesh axis runs over, the one named last changes fastest.
Arguments:
- query_proj: bfloat16 [16, 3072, 1024], P('dp', 'seq'), may hold values from -6 to 6
- key_proj: bfloat16 [16, 3072, 1024], P('dp', 'seq'), may hold values from -6 to 6
- value_proj: bfloat16 [16, 3072, 1024], P('dp', 'seq'), may hold values from -6 to 6
- cotangent: bfloat16 [16, 3072, 1024], P('dp', 'seq'), may hold values from -6 to 6
- out_weight: bfloat16 [1024, 1024], replicated, may hold values from -0.1875 to 0.1875
- conv_weight: float32 [31, 1024], replicated, may hold values from -1 to 1
- rec_starts: int32 [16, 2], P('dp'), may hold values from 0 to 3064, as said below
Outputs:
- layer_out: bfloat16 [16, 3072, 1024], P('dp', 'seq')
- query_grad: bfloat16 [16, 3072, 1024], P('dp', 'seq')
- key_grad: bfloat16 [16, 3072, 1024], P('dp', 'seq')
- value_grad: bfloat16 [16, 3072, 1024], P('dp', 'seq')
- weight_grad: float32 [1024, 1024], replicated
- conv_grad: float32 [31, 1024], replicated
Inputs may be any that keep to these rules, and one draw needn't show every extreme that they name: `rec_starts`: in each group the first start is 0, the starts rise strictly and each is a multiple of 8; a recording runs up to the next start, the last one to frame 3072 - 1.
All inputs are finite; a program needn't handle non-finite values.
Results may differ from a plain program's by a relative error of at most 0.02.
Values may be sent and summed in bfloat16 or wider, within the bound.
A program may use at most 64 MiB of HBM per device.

v0:
```python
import math

import jax
import jax.numpy as jnp
from jax import lax
from jax.sharding import PartitionSpec as P

HEAD_DIM = 64
KERN = 31
LAG = 30


def shifted(value, axis, steps):
    count = lax.axis_size(axis)
    leading, last = (max(0, -steps), min(count, count - steps))
    return lax.ppermute(value, axis, [(source, source + steps) for source in range(leading, last)])


def record_ids(frames, starts_row, total):
    above = (frames[:, None] >= starts_row[None, :]).astype(jnp.int32)
    labels = jnp.sum(above, axis=1) - 1
    inside = (frames >= 0) & (frames < total)
    return jnp.where(inside, labels, -2)


def depthwise(padded, labels_pad, labels_out, weights, count):
    total = jnp.zeros((count, padded.shape[1]), jnp.float32)
    for tap in range(weights.shape[0]):
        window = padded[tap : tap + count].astype(jnp.float32)
        same = (labels_pad[tap : tap + count] == labels_out)[:, None]
        total = total + jnp.where(same, weights[tap][None, :] * window, 0.0)
    return total


def transposed(padded, labels_pad, labels_out, weights, count):
    total = jnp.zeros((count, padded.shape[1]), jnp.float32)
    last = weights.shape[0] - 1
    for tap in range(weights.shape[0]):
        offset = last - tap
        window = padded[offset : offset + count].astype(jnp.float32)
        same = (labels_pad[offset : offset + count] == labels_out)[:, None]
        total = total + jnp.where(same, weights[tap][None, :] * window, 0.0)
    return total


def tap_sums(signal, padded, labels_pad, labels_out, taps):
    count = signal.shape[0]
    rows_out = []
    for tap in range(taps):
        window = padded[tap : tap + count].astype(jnp.float32)
        same = (labels_pad[tap : tap + count] == labels_out)[:, None]
        rows_out.append(jnp.sum(jnp.where(same, signal * window, 0.0), axis=0))
    return jnp.stack(rows_out)


def silu_parts(conv):
    gate_value = jax.nn.sigmoid(conv)
    return (conv * gate_value, gate_value * (1.0 + conv * (1.0 - gate_value)))


def block_scores(query_blk, key_part, labels_q, labels_k, scale):
    raw = (
        jnp.einsum("qhd,khd->hqk", query_blk, key_part, preferred_element_type=jnp.float32) * scale
    )
    same = (labels_q[:, None] == labels_k[None, :])[None]
    return jnp.where(same, raw, -1e30)


def block_grads(
    query_blk, key_part, value_part, mixed_blk, back_blk, labels_q, labels_k, norm_blk, scale
):
    scores = block_scores(query_blk, key_part, labels_q, labels_k, scale)
    probs = jnp.exp(scores - norm_blk[:, :, None]).astype(jnp.bfloat16)
    prob_back = jnp.einsum("qhd,khd->hqk", back_blk, value_part, preferred_element_type=jnp.float32)
    delta = jnp.sum(back_blk.astype(jnp.float32) * mixed_blk.astype(jnp.float32), axis=2).T
    score_back = (probs.astype(jnp.float32) * (prob_back - delta[:, :, None])).astype(jnp.bfloat16)
    return (probs, score_back)


def forward_dense(heads_q, heads_k, heads_v, labels, width, scale):
    total, heads_here, features = heads_q.shape
    count = total // width

    def forward_one_block(index):
        start = index * width
        query_blk = lax.dynamic_slice_in_dim(heads_q, start, width, 0)
        labels_q = lax.dynamic_slice_in_dim(labels, start, width, 0)
        scores = block_scores(query_blk, heads_k, labels_q, labels, scale)
        top = jnp.max(scores, axis=2, keepdims=True)
        norm = top + jnp.log(jnp.sum(jnp.exp(scores - top), axis=2, keepdims=True))
        probs = jnp.exp(scores - norm).astype(jnp.bfloat16)
        mixed_blk = jnp.einsum("hqk,khd->qhd", probs, heads_v, preferred_element_type=jnp.float32)
        return (mixed_blk.astype(jnp.bfloat16), norm[:, :, 0])

    mixed_blocks, norm_blocks = lax.map(forward_one_block, jnp.arange(count, dtype=jnp.int32))
    mixed_heads = mixed_blocks.reshape(total, heads_here, features)
    norms = norm_blocks.transpose(1, 0, 2).reshape(heads_here, total)
    return (mixed_heads, norms)


def backward_dense(heads_q, heads_k, heads_v, mixed_heads, back_heads, norms, labels, width, scale):
    total = heads_q.shape[0]
    count = total // width
    empty = jnp.zeros(heads_k.shape, jnp.float32)

    def backward_one_block(carry, index):
        key_acc, value_acc = carry
        start = index * width
        query_blk = lax.dynamic_slice_in_dim(heads_q, start, width, 0)
        mixed_blk = lax.dynamic_slice_in_dim(mixed_heads, start, width, 0)
        back_blk = lax.dynamic_slice_in_dim(back_heads, start, width, 0)
        labels_q = lax.dynamic_slice_in_dim(labels, start, width, 0)
        norm_blk = lax.dynamic_slice_in_dim(norms, start, width, 1)
        probs, score_back = block_grads(
            query_blk, heads_k, heads_v, mixed_blk, back_blk, labels_q, labels, norm_blk, scale
        )
        query_part = scale * jnp.einsum(
            "hqk,khd->qhd", score_back, heads_k, preferred_element_type=jnp.float32
        )
        key_acc = key_acc + scale * jnp.einsum(
            "hqk,qhd->khd", score_back, query_blk, preferred_element_type=jnp.float32
        )
        value_acc = value_acc + jnp.einsum(
            "hqk,qhd->khd", probs, back_blk, preferred_element_type=jnp.float32
        )
        return ((key_acc, value_acc), query_part.astype(jnp.bfloat16))

    sums, query_blocks = lax.scan(
        backward_one_block, (empty, empty), jnp.arange(count, dtype=jnp.int32)
    )
    query_grads = query_blocks.reshape(heads_q.shape)
    return (query_grads, sums[0].astype(jnp.bfloat16), sums[1].astype(jnp.bfloat16))


def local(query_proj, key_proj, value_proj, cotangent, out_weight, conv_weight, rec_starts):
    rows = query_proj.shape[1]
    parts = lax.axis_size("seq")
    place = lax.axis_index("seq")
    total = rows * parts
    width = min(512, total)
    scale = HEAD_DIM ** (-0.5)
    starts_row = rec_starts[0]
    sent = (
        lax.all_to_all(query_proj[0], "seq", split_axis=1, concat_axis=0, tiled=True),
        lax.all_to_all(key_proj[0], "seq", split_axis=1, concat_axis=0, tiled=True),
        lax.all_to_all(value_proj[0], "seq", split_axis=1, concat_axis=0, tiled=True),
    )
    heads_q = sent[0].reshape(total, -1, HEAD_DIM)
    heads_k = sent[1].reshape(total, -1, HEAD_DIM)
    heads_v = sent[2].reshape(total, -1, HEAD_DIM)
    labels = record_ids(jnp.arange(total, dtype=jnp.int32), starts_row, total)
    mixed_heads, norms = forward_dense(heads_q, heads_k, heads_v, labels, width, scale)
    mixed_rows = lax.all_to_all(
        mixed_heads.reshape(total, -1), "seq", split_axis=0, concat_axis=1, tiled=True
    )
    projected = jnp.dot(mixed_rows, out_weight, preferred_element_type=jnp.float32).astype(
        jnp.bfloat16
    )
    labels_local = record_ids(place * rows + jnp.arange(rows, dtype=jnp.int32), starts_row, total)
    cot = cotangent[0]
    behind = shifted(projected[rows - LAG :], "seq", 1)
    padded = jnp.concatenate([behind, projected], axis=0)
    labels_pad = record_ids(
        place * rows - LAG + jnp.arange(rows + LAG, dtype=jnp.int32), starts_row, total
    )
    labels_back = record_ids(
        place * rows + jnp.arange(rows + LAG, dtype=jnp.int32), starts_row, total
    )
    conv = depthwise(padded, labels_pad, labels_local, conv_weight, rows)
    activated, slope = silu_parts(conv)
    conv_back = cot.astype(jnp.float32) * slope
    ahead_back = shifted(conv_back[:LAG].astype(jnp.bfloat16), "seq", -1).astype(jnp.float32)
    back_pad = jnp.concatenate([conv_back, ahead_back], axis=0)
    layer_out = (projected.astype(jnp.float32) + activated).astype(jnp.bfloat16)
    spread = transposed(back_pad, labels_back, labels_local, conv_weight, rows)
    proj_back = (cot.astype(jnp.float32) + spread).astype(jnp.bfloat16)
    conv_local = tap_sums(conv_back, padded, labels_pad, labels_local, KERN)
    factor = 1.0 / math.sqrt(lax.axis_size("dp") * total)
    weight_local = lax.dot_general(
        mixed_rows, proj_back, (((0,), (0,)), ((), ())), preferred_element_type=jnp.float32
    )
    summed = lax.psum((weight_local, conv_local), ("dp", "seq"))
    weight_grad = summed[0] * factor
    conv_grad = summed[1] * factor
    mixed_back = lax.dot_general(
        proj_back, out_weight, (((1,), (1,)), ((), ())), preferred_element_type=jnp.float32
    ).astype(jnp.bfloat16)
    back_heads = lax.all_to_all(mixed_back, "seq", split_axis=1, concat_axis=0, tiled=True).reshape(
        total, -1, HEAD_DIM
    )
    grad_q, grad_k, grad_v = backward_dense(
        heads_q, heads_k, heads_v, mixed_heads, back_heads, norms, labels, width, scale
    )
    returned = (
        lax.all_to_all(grad_q.reshape(total, -1), "seq", split_axis=0, concat_axis=1, tiled=True),
        lax.all_to_all(grad_k.reshape(total, -1), "seq", split_axis=0, concat_axis=1, tiled=True),
        lax.all_to_all(grad_v.reshape(total, -1), "seq", split_axis=0, concat_axis=1, tiled=True),
    )
    return (
        layer_out[None],
        returned[0][None],
        returned[1][None],
        returned[2][None],
        weight_grad,
        conv_grad,
    )


def solution(mesh):
    return jax.shard_map(
        local,
        mesh=mesh,
        in_specs=(
            P("dp", "seq", None),
            P("dp", "seq", None),
            P("dp", "seq", None),
            P("dp", "seq", None),
            P(),
            P(),
            P("dp", None),
        ),
        out_specs=(
            P("dp", "seq", None),
            P("dp", "seq", None),
            P("dp", "seq", None),
            P("dp", "seq", None),
            P(),
            P(),
        ),
        check_vma=False,
    )
```

profile of v0, /device:TPU:1, one launch (start us, length us, event | category | flops | bytes accessed | tf_op | source)
XLA Modules:
  0.0 610.6 jit_solution(17486042419321726274)
XLA Ops:
  9.3 10.0 %all-to-all-start = ((bf16[192,16,64]{0,2,1:T(8,128)(2,1)}), bf16[192,16,64]{0,2,1:T(8,128)(2,1)S(1)}, u32[]{:S(2)}, u32[]{:S(2)}) async-start(bf16[192,16,64]{0,2,1:T(8,128)(2,1)} %bitcast.10), calls=%async_computation | async-start | bytes 1048576 | tf_op jit(solution)/shard_map/all_to_all | solution.py:144
  23.3 13.3 %all-to-all-done = bf16[192,16,64]{0,2,1:T(8,128)(2,1)S(1)} async-done(((bf16[192,16,64]{0,2,1:T(8,128)(2,1)}), bf16[192,16,64]{0,2,1:T(8,128)(2,1)S(1)}, u32[]{:S(2)}, u32[]{:S(2)}) %all-to-all-start) | async-done | bytes 393248 | tf_op jit(solution)/shard_map/all_to_all | solution.py:144
  36.6 3.5 all-to-all-start.1
  41.6 15.2 %all-to-all-done.1 = bf16[192,16,64]{0,2,1:T(8,128)(2,1)S(1)} async-done(((bf16[192,16,64]{0,2,1:T(8,128)(2,1)}), bf16[192,16,64]{0,2,1:T(8,128)(2,1)S(1)}, u32[]{:S(2)}, u32[]{:S(2)}) %all-to-all-start.1) | async-done | bytes 393248 | tf_op jit(solution)/shard_map/all_to_all | solution.py:145
  56.8 4.1 all-to-all-start.2
  66.5 10.6 %all-to-all-done.2 = bf16[192,16,64]{0,2,1:T(8,128)(2,1)} async-done(((bf16[192,16,64]{0,2,1:T(8,128)(2,1)}), bf16[192,16,64]{0,2,1:T(8,128)(2,1)}, u32[]{:S(2)}, u32[]{:S(2)}) %all-to-all-start.2) | async-done | bytes 393248 | tf_op jit(solution)/shard_map/all_to_all | solution.py:146
  79.1 37.1 %while.27 = (s32[]{:T(128)}, bf16[6,512,1,64]{1,3,2,0:T(8,128)(2,1)S(1)}, f32[6,1,512]{2,1,0:T(1,128)}, s32[6]{0:T(128)S(1)}, s32[3072]{0:T(1024)S(1)}, /*index=...) while((s32[]{:T(128)}, ...), condition=%wide.region_4.5_spmd, body=%wide.region_1.4_spmd.sunk | while | flops 415268352 | bytes 19828936 | solution.py:95
  121.7 3.5 all-to-all-start.3
  130.4 11.5 %all-to-all-done.3 = bf16[16,192,64]{1,2,0:T(8,128)(2,1)S(1)} async-done(((bf16[16,192,64]{1,2,0:T(8,128)(2,1)}), bf16[16,192,64]{1,2,0:T(8,128)(2,1)S(1)}, u32[]{:S(2)}, u32[]{:S(2)}) %all-to-all-start.3) | async-done | bytes 393248 | tf_op jit(solution)/shard_map/all_to_all | solution.py:153
  149.1 19.4 %fusion.155 = (f32[1024]{0:T(1024)S(1)}, f32[192,1024]{1,0:T(8,128)S(1)}, f32[192,1024]{1,0:T(8,128)}) fusion(bf16[192,1024]{1,0:T(8,128)(2,1)} %copy-done.1, pred[192]{0:T(512)(128)(4,1)} %get-tuple-element.318, bf16[1,192,1024]{2,1,0:T(8,128)(2,1)} %param.14, f32[1024]{0:T(1024)} %bitcast.257, bf16[30,1024]{1,0:T(8,128)(2,1)S(1)} %collective-permute-done, ...), kind=kLoop, calls=%fused_computation.322 | loop fusion | flops 44235776 | bytes 2557760 | tf_op jit(solution)/shard_map/reduce_sum | solution.py:52
  171.0 3.9 fusion.90
  174.9 4.0 fusion.108
  182.0 9.1 %fusion.151 = bf16[192,1024]{1,0:T(8,128)(2,1)S(1)} fusion(f32[192,1024]{1,0:T(8,128)S(1)} %get-tuple-element.250, f32[30,1024]{1,0:T(8,128)S(1)} %convert_element_type.251, bf16[1,192,1024]{2,1,0:T(8,128)(2,1)S(1)} %copy-done.15, f32[1024]{0:T(1024)S(1)} %bitcast.258, f32[1024]{0:T(1024)S(1)} %bitcast.260, f32[1024]{0:T(1024)S(1)} %bitcast.264, ...), kind=kLoop, calls=%fused_computation.318 | loop fusion | flops 24576000 | bytes 1828672 | tf_op jit(solution)/shard_map/convert_element_type | solution.py:176
  195.5 5.4 all-to-all-start.4
  200.9 4.1 fusion.150
  205.0 4.2 fusion.126
  211.9 6.5 %all-to-all-done.4 = bf16[192,16,64]{0,2,1:T(8,128)(2,1)} async-done(((bf16[192,16,64]{0,2,1:T(8,128)(2,1)}), bf16[192,16,64]{0,2,1:T(8,128)(2,1)}, u32[]{:S(2)}, u32[]{:S(2)}) %all-to-all-start.4) | async-done | bytes 393248 | tf_op jit(solution)/shard_map/all_to_all | solution.py:188
  221.7 82.6 %while.28 = (s32[]{:T(128)}, f32[3072,1,64]{0,2,1:T(8,128)}, f32[3072,1,64]{0,2,1:T(8,128)}, bf16[6,512,1,64]{1,3,2,0:T(8,128)(2,1)}, s32[6]{0:T(128)S(1)}, /*in...) while((s32[]{:T(128)}, f32[3072,1,64]{0,2,1:T(8,128)}, ...), condition=%wide.region_10.11_spmd.clone, body=%wide.region_8.10_spmd.clone.sunk | while | flops 1021967872 | bytes 37843340 | solution.py:128
  224.8 2.7 exponential_convert_fusion.12
  238.5 2.8 exponential_convert_fusion.12
  252.3 2.7 exponential_convert_fusion.12
  266.0 2.7 exponential_convert_fusion.12
  279.8 2.8 exponential_convert_fusion.12
  307.1 4.1 all-to-all-start.5
  311.3 3.9 fusion.313
  321.7 5.8 all-to-all-done.5
  327.4 4.1 all-to-all-start.6
  335.0 14.7 %all-to-all-done.6 = bf16[16,192,64]{1,2,0:T(8,128)(2,1)} async-done(((bf16[16,192,64]{1,2,0:T(8,128)(2,1)}), bf16[16,192,64]{1,2,0:T(8,128)(2,1)}, u32[]{:S(2)}, u32[]{:S(2)}) %all-to-all-start.6) | async-done | bytes 393248 | tf_op jit(solution)/shard_map/all_to_all | solution.py:196
  349.7 3.5 all-to-all-start.7
  359.3 12.1 %all-to-all-done.7 = bf16[16,192,64]{1,2,0:T(8,128)(2,1)S(1)} async-done(((bf16[16,192,64]{1,2,0:T(8,128)(2,1)}), bf16[16,192,64]{1,2,0:T(8,128)(2,1)S(1)}, u32[]{:S(2)}, u32[]{:S(2)}) %all-to-all-start.7) | async-done | bytes 393248 | tf_op jit(solution)/shard_map/all_to_all | solution.py:197
  372.3 225.6 %all-reduce.3.cloned.1.call-done = (f32[1024,1024]{1,0:T(8,128)}, f32[31,1024]{1,0:T(8,128)}) async-done(((f32[1024,1024]{1,0:T(8,128)}, f32[31,1024]{1,0:T(8,128)}), (f32[1024,1024]{1,0:T(8,128)}, f32[31,1024]{1,0:T(8,128)})) %all-reduce.3.cloned.1.call-update) | async-done | bytes 4321296 | tf_op jit(solution)/shard_map/psum | solution.py:182
  597.9 5.2 broadcast_multiply_fusion
  (324 shorter events, 165.8 us)
Async XLA Ops:
  7.2 134.8 %copy-start = (bf16[1024,1024]{1,0:T(8,128)(2,1)S(1)}, bf16[1024,1024]{1,0:T(8,128)(2,1)}, u32[]{:S(2)}) copy-start(bf16[1024,1024]{1,0:T(8,128)(2,1)} %param.15) | copy-start | bytes 6291460
  9.3 27.3 %all-to-all-start = ((bf16[192,16,64]{0,2,1:T(8,128)(2,1)}), bf16[192,16,64]{0,2,1:T(8,128)(2,1)S(1)}, u32[]{:S(2)}, u32[]{:S(2)}) async-start(bf16[192,16,64]{0,2,1:T(8,128)(2,1)} %bitcast.10), calls=%async_computation | async-start | bytes 1048576 | tf_op jit(solution)/shard_map/all_to_all | solution.py:144
  36.6 20.2 %all-to-all-start.1 = ((bf16[192,16,64]{0,2,1:T(8,128)(2,1)}), bf16[192,16,64]{0,2,1:T(8,128)(2,1)S(1)}, u32[]{:S(2)}, u32[]{:S(2)}) async-start(bf16[192,16,64]{0,2,1:T(8,128)(2,1)} %bitcast.12), calls=%async_computation.1 | async-start | bytes 1048576 | tf_op jit(solution)/shard_map/all_to_all | solution.py:145
  56.8 20.4 %all-to-all-start.2 = ((bf16[192,16,64]{0,2,1:T(8,128)(2,1)}), bf16[192,16,64]{0,2,1:T(8,128)(2,1)}, u32[]{:S(2)}, u32[]{:S(2)}) async-start(bf16[192,16,64]{0,2,1:T(8,128)(2,1)} %bitcast.14), calls=%async_computation.2 | async-start | bytes 1048576 | tf_op jit(solution)/shard_map/all_to_all | solution.py:146
  62.3 63.6 %copy-start.48 = (s32[192]{0:T(256)}, s32[192]{0:T(256)S(1)}, u32[]{:S(2)}) copy-start(s32[192]{0:T(256)S(1)} %get-tuple-element.253) | copy-start | bytes 2308
  121.7 20.2 %all-to-all-start.3 = ((bf16[16,192,64]{1,2,0:T(8,128)(2,1)}), bf16[16,192,64]{1,2,0:T(8,128)(2,1)S(1)}, u32[]{:S(2)}, u32[]{:S(2)}) async-start(bf16[16,192,64]{1,2,0:T(8,128)(2,1)} %copy.63), calls=%async_computation.3 | async-start | bytes 1048576 | tf_op jit(solution)/shard_map/all_to_all | solution.py:153
  143.3 5.8 collective-permute-start
  146.8 34.8 %copy-start.17 = (f32[1,1024]{1,0:T(1,128)S(1)}, f32[1,1024]{1,0:T(1,128)}, u32[]{:S(2)}) copy-start(f32[1,1024]{1,0:T(1,128)} %get-tuple-element.275) | copy-start | bytes 12292
  146.8 34.8 %copy-start.15 = (bf16[1,192,1024]{2,1,0:T(8,128)(2,1)S(1)}, bf16[1,192,1024]{2,1,0:T(8,128)(2,1)}, u32[]{:S(2)}) copy-start(bf16[1,192,1024]{2,1,0:T(8,128)(2,1)} %param.14) | copy-start | bytes 1179652
  146.8 34.8 %copy-start.18 = (f32[1,1024]{1,0:T(1,128)S(1)}, f32[1,1024]{1,0:T(1,128)}, u32[]{:S(2)}) copy-start(f32[1,1024]{1,0:T(1,128)} %get-tuple-element.276) | copy-start | bytes 12292
  146.9 34.8 %copy-start.19 = (f32[1,1024]{1,0:T(1,128)S(1)}, f32[1,1024]{1,0:T(1,128)}, u32[]{:S(2)}) copy-start(f32[1,1024]{1,0:T(1,128)} %get-tuple-element.277) | copy-start | bytes 12292
  146.9 34.8 %copy-start.20 = (f32[1,1024]{1,0:T(1,128)S(1)}, f32[1,1024]{1,0:T(1,128)}, u32[]{:S(2)}) copy-start(f32[1,1024]{1,0:T(1,128)} %get-tuple-element.278) | copy-start | bytes 12292
  146.9 34.8 %copy-start.21 = (f32[1,1024]{1,0:T(1,128)S(1)}, f32[1,1024]{1,0:T(1,128)}, u32[]{:S(2)}) copy-start(f32[1,1024]{1,0:T(1,128)} %get-tuple-element.279) | copy-start | bytes 12292
  146.9 34.8 %copy-start.22 = (f32[1,1024]{1,0:T(1,128)S(1)}, f32[1,1024]{1,0:T(1,128)}, u32[]{:S(2)}) copy-start(f32[1,1024]{1,0:T(1,128)} %get-tuple-element.280) | copy-start | bytes 12292
  146.9 34.8 %copy-start.23 = (f32[1,1024]{1,0:T(1,128)S(1)}, f32[1,1024]{1,0:T(1,128)}, u32[]{:S(2)}) copy-start(f32[1,1024]{1,0:T(1,128)} %get-tuple-element.281) | copy-start | bytes 12292
  146.9 34.8 %copy-start.24 = (f32[1,1024]{1,0:T(1,128)S(1)}, f32[1,1024]{1,0:T(1,128)}, u32[]{:S(2)}) copy-start(f32[1,1024]{1,0:T(1,128)} %get-tuple-element.282) | copy-start | bytes 12292
  146.9 34.8 %copy-start.25 = (f32[1,1024]{1,0:T(1,128)S(1)}, f32[1,1024]{1,0:T(1,128)}, u32[]{:S(2)}) copy-start(f32[1,1024]{1,0:T(1,128)} %get-tuple-element.283) | copy-start | bytes 12292
  146.9 34.8 %copy-start.26 = (f32[1,1024]{1,0:T(1,128)S(1)}, f32[1,1024]{1,0:T(1,128)}, u32[]{:S(2)}) copy-start(f32[1,1024]{1,0:T(1,128)} %get-tuple-element.284) | copy-start | bytes 12292
  146.9 34.8 %copy-start.27 = (f32[1,1024]{1,0:T(1,128)S(1)}, f32[1,1024]{1,0:T(1,128)}, u32[]{:S(2)}) copy-start(f32[1,1024]{1,0:T(1,128)} %get-tuple-element.285) | copy-start | bytes 12292
  146.9 34.8 %copy-start.28 = (f32[1,1024]{1,0:T(1,128)S(1)}, f32[1,1024]{1,0:T(1,128)}, u32[]{:S(2)}) copy-start(f32[1,1024]{1,0:T(1,128)} %get-tuple-element.286) | copy-start | bytes 12292
  147.0 34.8 %copy-start.29 = (f32[1,1024]{1,0:T(1,128)S(1)}, f32[1,1024]{1,0:T(1,128)}, u32[]{:S(2)}) copy-start(f32[1,1024]{1,0:T(1,128)} %get-tuple-element.256) | copy-start | bytes 12292
  147.0 34.8 %copy-start.30 = (f32[1,1024]{1,0:T(1,128)S(1)}, f32[1,1024]{1,0:T(1,128)}, u32[]{:S(2)}) copy-start(f32[1,1024]{1,0:T(1,128)} %get-tuple-element.257) | copy-start | bytes 12292
  147.0 34.8 %copy-start.31 = (f32[1,1024]{1,0:T(1,128)S(1)}, f32[1,1024]{1,0:T(1,128)}, u32[]{:S(2)}) copy-start(f32[1,1024]{1,0:T(1,128)} %get-tuple-element.258) | copy-start | bytes 12292
  147.0 34.8 %copy-start.32 = (f32[1,1024]{1,0:T(1,128)S(1)}, f32[1,1024]{1,0:T(1,128)}, u32[]{:S(2)}) copy-start(f32[1,1024]{1,0:T(1,128)} %get-tuple-element.259) | copy-start | bytes 12292
  147.0 34.8 %copy-start.33 = (f32[1,1024]{1,0:T(1,128)S(1)}, f32[1,1024]{1,0:T(1,128)}, u32[]{:S(2)}) copy-start(f32[1,1024]{1,0:T(1,128)} %get-tuple-element.260) | copy-start | bytes 12292
  168.6 13.0 %collective-permute-start.1 = (bf16[30,1024]{1,0:T(8,128)(2,1)S(1)}, bf16[30,1024]{1,0:T(8,128)(2,1)S(1)}, u32[]{:S(2)}, u32[]{:S(2)}) collective-permute-start(bf16[30,1024]{1,0:T(8,128)(2,1)S(1)} %slice.1694), channel_id=1, source_target_pairs={{1,0},{2,1},{3,2},{4,3},{5,4},{6,5},{7,6},{8,7},{9,8},{10,9},{11,1... | collective-permute-start | bytes 184328 | tf_op jit(solution)/shard_map/ppermute | solution.py:16
  195.5 22.8 %all-to-all-start.4 = ((bf16[192,16,64]{0,2,1:T(8,128)(2,1)}), bf16[192,16,64]{0,2,1:T(8,128)(2,1)}, u32[]{:S(2)}, u32[]{:S(2)}) async-start(bf16[192,16,64]{0,2,1:T(8,128)(2,1)} %bitcast.230), calls=%async_computation.4 | async-start | bytes 1048576 | tf_op jit(solution)/shard_map/all_to_all | solution.py:188
  307.1 20.3 %all-to-all-start.5 = ((bf16[16,192,64]{1,2,0:T(8,128)(2,1)}), bf16[16,192,64]{1,2,0:T(8,128)(2,1)}, u32[]{:S(2)}, u32[]{:S(2)}) async-start(bf16[16,192,64]{1,2,0:T(8,128)(2,1)} %copy.68), calls=%async_computation.5 | async-start | bytes 1048576 | tf_op jit(solution)/shard_map/all_to_all | solution.py:195
  311.3 286.6 %all-reduce.3.cloned.1.call-start = ((), (), s32[]{:S(2)}) async-start(), calls=%async_computation.8 | async-start | bytes 8650752 | tf_op jit(solution)/shard_map/psum | solution.py:182
  315.2 37.9 %copy-start.3 = (bf16[192,1024]{1,0:T(8,128)(2,1)S(1)}, bf16[192,1024]{1,0:T(8,128)(2,1)}, u32[]{:S(2)}) copy-start(bf16[192,1024]{1,0:T(8,128)(2,1)} %copy-done.1) | copy-start | bytes 1179652
  327.4 22.3 %all-to-all-start.6 = ((bf16[16,192,64]{1,2,0:T(8,128)(2,1)}), bf16[16,192,64]{1,2,0:T(8,128)(2,1)}, u32[]{:S(2)}, u32[]{:S(2)}) async-start(bf16[16,192,64]{1,2,0:T(8,128)(2,1)} %copy.69), calls=%async_computation.6 | async-start | bytes 1048576 | tf_op jit(solution)/shard_map/all_to_all | solution.py:196
  349.7 21.7 %all-to-all-start.7 = ((bf16[16,192,64]{1,2,0:T(8,128)(2,1)}), bf16[16,192,64]{1,2,0:T(8,128)(2,1)S(1)}, u32[]{:S(2)}, u32[]{:S(2)}) async-start(bf16[16,192,64]{1,2,0:T(8,128)(2,1)} %copy.70), calls=%async_computation.7 | async-start | bytes 1048576 | tf_op jit(solution)/shard_map/all_to_all | solution.py:197
  (63 other events, 1010.1 us)
Sparse Core Ops, SparseCore 0:
  318.2 279.6 all-reduce.2
where the time goes:
time: 615 us; the launch traced here: 611 us
  waiting for transfers between devices  315 us (51%)
  matrix products  84.2 us (14%)
  other arithmetic  76 us (12%)
  local copies, waits for them, and re-layouts  68.6 us (11%)
  starting transfers between devices  42.8 us (7%)
  between operations  15 us (2%)
  loops' own time  8.71 us (1%)
    psum x1, waiting for transfers between devices, local(): summed = lax.psum((weight_local, conv_local), ('dp', 'seq'))  226 us
    reduce_sum x6, other arithmetic, tap_sums(): rows_out.append(jnp.sum(jnp.where(same, signal * window, 0.0), axis=0))  38.3 us
    dot_general x12, matrix products, block_scores(): jnp.einsum('qhd,khd->hqk', query_blk, key_part, preferred_element_type=jn...  28.9 us
    all_to_all x1, waiting for transfers between devices, local(): lax.all_to_all(key_proj[0], 'seq', split_axis=1, concat_axis=0, tiled=True)  15.2 us
    all_to_all x1, waiting for transfers between devices, local(): lax.all_to_all(grad_k.reshape(total, -1), 'seq', split_axis=0, concat_axi...  14.7 us
    all_to_all x1, waiting for transfers between devices, local(): lax.all_to_all(query_proj[0], 'seq', split_axis=1, concat_axis=0, tiled=T...  13.3 us
    unnamed x114, local copies, waits for them, and re-layouts  12.8 us
  transfers between devices with their start and end apart: 11, of which 9 were waited for; matrix products, arithmetic and copies ran while one was open for 9% of the time, Pallas kernels for 0%

commit v1 on v0

v1 whole, which is shorter than its diff:
```python
import functools

import jax
import jax.numpy as jnp
from jax import lax
from jax.experimental import pallas as pl
from jax.experimental.pallas import tpu as pltpu
from jax.sharding import PartitionSpec as P

HD = 64
KERN = 31
HALO = 32
BLK = 256
SUB = 3
BIG = 1e30
BF = jnp.bfloat16
F32 = jnp.float32
VM = pl.BlockSpec(memory_space=pltpu.VMEM)
SM = pl.BlockSpec(memory_space=pltpu.SMEM)
ANY = pl.BlockSpec(memory_space=pl.ANY)


def dot(a, b, ca=1, cb=0):
    return lax.dot_general(a, b, (((ca,), (cb,)), ((), ())), preferred_element_type=F32)


def low_lanes(rows):
    return lax.broadcasted_iota(jnp.int32, (rows, 128), 1) < HD


def swap(x):
    return pltpu.roll(x, HD, 1)


def pack_halves(x):
    half = x.shape[0] // 2
    low = low_lanes(half)
    top, bottom = x[:half], x[half:]
    return jnp.where(low, top, swap(bottom)), jnp.where(low, swap(top), bottom)


def unpack_halves(first, second):
    low = low_lanes(first.shape[0])
    return jnp.where(low, first, swap(second)), jnp.where(low, swap(first), second)


def greet(axes):
    barrier = pltpu.get_barrier_semaphore()
    total = 0
    for axis in axes:
        count = lax.axis_size(axis)
        me = lax.axis_index(axis)

        def signal(d, _, axis=axis, count=count, me=me):
            pl.semaphore_signal(barrier, inc=1, device_id={axis: lax.rem(me + d, count)})
            return 0

        lax.fori_loop(1, count, signal, 0)
        total += count - 1
    pl.semaphore_wait(barrier, total)


def rows_at(index, size):
    return pl.ds(pl.multiple_of(index * size, size), size)


def fwd_kernel(
    starts, q_ref, k_ref, v_ref,
    p_out, kf_out, qf_out, kt_out, aux_out, mixed_out,
    kv_send, q_send, kf, q_recv, qf, kt, vt, s_buf, p_buf, aux, mix_send, mix_recv,
    kv_ss, kv_rs, q_ss, q_rs, m_ss, m_rs, p_sem, o_sem,
):
    n = lax.axis_size("seq")
    me = lax.axis_index("seq")
    rows, width = q_ref.shape
    half = rows // 2
    total = n * rows
    chunks = total // BLK
    group = SUB * BLK
    groups = total // group
    owners = group // rows
    for t in range(width // 128):
        cols = pl.ds(t * 128, 128)
        kt_, vt_ = k_ref[:, cols].astype(F32), v_ref[:, cols].astype(F32)
        low = low_lanes(rows)
        kv_send[2 * t] = jnp.where(low, kt_, swap(vt_)).astype(BF)
        kv_send[2 * t + 1] = jnp.where(low, swap(kt_), vt_).astype(BF)
        first, second = pack_halves(q_ref[:, cols].astype(F32) * (HD**-0.5))
        q_send[2 * t] = first.astype(BF)
        q_send[2 * t + 1] = second.astype(BF)
    greet(("seq",))

    def kv_copy(peer, owner, dst_dev):
        return pltpu.make_async_remote_copy(
            src_ref=kv_send.at[peer],
            dst_ref=kf.at[rows_at(owner, rows), pl.ds(0, 128)],
            send_sem=kv_ss.at[peer],
            recv_sem=kv_rs.at[owner],
            device_id={"seq": dst_dev},
        )

    def q_copy(peer, owner, dst_dev):
        return pltpu.make_async_remote_copy(
            src_ref=q_send.at[peer],
            dst_ref=q_recv.at[owner],
            send_sem=q_ss.at[peer],
            recv_sem=q_rs.at[owner],
            device_id={"seq": dst_dev},
        )

    def start(d, _):
        peer = lax.rem(me + d, n)
        kv_copy(peer, me, peer).start()
        q_copy(peer, me, peer).start()
        return 0

    lax.fori_loop(1, n, start, 0)
    kf[rows_at(me, rows), pl.ds(0, 128)] = kv_send[me]
    q_recv[me] = q_send[me]
    second = starts[0, 1]

    def feats(i, _):
        at = lax.broadcasted_iota(jnp.int32, (BLK, 128), 0) + i * BLK
        lane = lax.broadcasted_iota(jnp.int32, (BLK, 128), 1)
        later = jnp.where(at >= second, 1.0, 0.0)
        own = jnp.where(lane == 0, 1.0 - later, jnp.where(lane == 1, later, 0.0))
        other = jnp.where(lane == 0, later, jnp.where(lane == 1, 1.0 - later, 0.0)) * (-BIG)
        ones = jnp.where((lane >= 2) & (lane < 5), 1.0, 0.0)
        kf[rows_at(i, BLK), pl.ds(128, 128)] = (other + ones).astype(BF)
        qf[rows_at(i, BLK), pl.ds(128, 128)] = own.astype(BF)
        return 0

    lax.fori_loop(0, chunks, feats, 0)

    def arrive(d, _):
        src = lax.rem(me - d + n, n)
        kv_copy(me, src, me).wait_recv()
        q_copy(me, src, me).wait_recv()
        return 0

    lax.fori_loop(1, n, arrive, 0)

    def unpack_q(p, _):
        x = q_recv[p].astype(F32)
        low = low_lanes(half)
        qf[rows_at(2 * p, half), pl.ds(0, 128)] = jnp.where(low, x, 0.0).astype(BF)
        qf[rows_at(2 * p + 1, half), pl.ds(0, 128)] = jnp.where(low, swap(x), 0.0).astype(BF)
        return 0

    lax.fori_loop(0, n, unpack_q, 0)
    vt[HD : HD + 16, :] = jnp.ones((16, total), BF)
    for c in range(chunks):
        x = kf[c * BLK : (c + 1) * BLK, 0:128].T
        kt[:, c * BLK : (c + 1) * BLK] = x[:HD]
        vt[0:HD, c * BLK : (c + 1) * BLK] = x[HD:]
    outs = [
        pltpu.make_async_copy(kf, kf_out, o_sem.at[0]),
        pltpu.make_async_copy(qf, qf_out, o_sem.at[1]),
        pltpu.make_async_copy(kt, kt_out, o_sem.at[2]),
    ]
    for copy in outs:
        copy.start()

    def scores(c, q_blk):
        return dot(kf[c * BLK : (c + 1) * BLK, :], q_blk, 1, 1)

    def col_max(best, s):
        return jnp.maximum(best, jnp.max(s.reshape(BLK // 8, 8, BLK), axis=0))

    first_group = me // (n // groups)
    low_start = jnp.full((8, BLK), -3e38, F32)
    q_blk = qf[rows_at(first_group * SUB, BLK), :]
    best = low_start
    for c in range(chunks):
        s = scores(c, q_blk)
        s_buf[0, c * BLK : (c + 1) * BLK, :] = s
        best = col_max(best, s)

    def p_copy(sub, at):
        return pltpu.make_async_copy(p_buf.at[sub], p_out.at[at], p_sem.at[sub])

    def mix_copy(peer, owner, dst_dev):
        return pltpu.make_async_remote_copy(
            src_ref=mix_send.at[peer],
            dst_ref=mix_recv.at[owner],
            send_sem=m_ss.at[peer],
            recv_sem=m_rs.at[owner],
            device_id={"seq": dst_dev},
        )

    def one_group(i, m):
        g = lax.rem(first_group + i, groups)
        g_next = lax.rem(first_group + i + 1, groups)
        for sub in range(SUB):
            at = g * SUB + sub
            ahead = (sub + 1) % SUB
            next_at = at + 1 if sub + 1 < SUB else g_next * SUB

            @pl.when(i > 0)
            def _():
                p_copy(sub, at).wait()

            q_next = qf[rows_at(next_at, BLK), :]
            best = low_start
            acc = jnp.zeros((HD + 16, BLK), F32)
            for c in range(chunks):
                cut = slice(c * BLK, (c + 1) * BLK)
                s = scores(c, q_next)
                s_buf[ahead, cut, :] = s
                best = col_max(best, s)
                p = jnp.exp(s_buf[sub, cut, :] - m).astype(BF)
                p_buf[sub, cut, :] = p
                acc = acc + dot(vt[:, cut], p)
            m = jnp.max(best, axis=0, keepdims=True)
            p_copy(sub, at).start()
            inverse = 1.0 / acc[HD : HD + 1]
            mixed = (acc[:HD] * inverse).astype(BF).astype(F32)
            both = jnp.concatenate([jnp.broadcast_to(inverse, (HD, BLK)), mixed], axis=0)
            aux[rows_at(at, BLK), :] = both.T
        for w in range(owners):
            owner = g * owners + w
            top = aux[rows_at(2 * owner, half), :]
            bottom = aux[rows_at(2 * owner + 1, half), :]
            packed = jnp.where(low_lanes(half), swap(top), bottom).astype(BF)
            mix_send[owner] = packed

            @pl.when(owner != me)
            def _():
                mix_copy(owner, me, owner).start()

            @pl.when(owner == me)
            def _():
                mix_recv[owner] = mix_send[owner]

        return m

    lax.fori_loop(0, groups, one_group, jnp.max(best, axis=0, keepdims=True))
    aux_copy = pltpu.make_async_copy(aux, aux_out, o_sem.at[3])
    aux_copy.start()

    def settle(d, _):
        peer = lax.rem(me + d, n)
        kv_copy(peer, me, peer).wait_send()
        q_copy(peer, me, peer).wait_send()
        mix_copy(peer, me, peer).wait_send()
        mix_copy(me, lax.rem(me - d + n, n), me).wait_recv()
        return 0

    lax.fori_loop(1, n, settle, 0)
    for t in range(width // 128):
        top, bottom = unpack_halves(mix_recv[2 * t].astype(F32), mix_recv[2 * t + 1].astype(F32))
        mixed_out[0:half, t * 128 : (t + 1) * 128] = top.astype(BF)
        mixed_out[half:rows, t * 128 : (t + 1) * 128] = bottom.astype(BF)
    for sub in range(SUB):
        p_copy(sub, 0).wait()
    for copy in outs:
        copy.wait()
    aux_copy.wait()


def forward(starts, q, k, v):
    rows, width = q.shape
    n = lax.axis_size("seq")
    total = n * rows
    half = rows // 2
    shape = jax.ShapeDtypeStruct
    dma = pltpu.SemaphoreType.DMA
    return pl.pallas_call(
        fwd_kernel,
        out_shape=[
            shape((total // BLK, total, BLK), BF),
            shape((total, 256), BF),
            shape((total, 256), BF),
            shape((HD, total), BF),
            shape((total, 128), F32),
            shape((rows, width), BF),
        ],
        in_specs=[SM, VM, VM, VM],
        out_specs=[ANY, ANY, ANY, ANY, ANY, VM],
        scratch_shapes=[
            pltpu.VMEM((n, rows, 128), BF),
            pltpu.VMEM((n, half, 128), BF),
            pltpu.VMEM((total, 256), BF),
            pltpu.VMEM((n, half, 128), BF),
            pltpu.VMEM((total, 256), BF),
            pltpu.VMEM((HD, total), BF),
            pltpu.VMEM((HD + 16, total), BF),
            pltpu.VMEM((SUB, total, BLK), F32),
            pltpu.VMEM((SUB, total, BLK), BF),
            pltpu.VMEM((total, 128), F32),
            pltpu.VMEM((n, half, 128), BF),
            pltpu.VMEM((n, half, 128), BF),
            dma((n,)), dma((n,)), dma((n,)), dma((n,)), dma((n,)), dma((n,)),
            dma((SUB,)), dma((4,)),
        ],
        compiler_params=pltpu.CompilerParams(
            collective_id=0, has_side_effects=True, vmem_limit_bytes=60 * 2**20
        ),
        name="attend",
    )(starts, q, k, v)


def conv_kernel(
    starts, mixed_ref, w_ref, cot_ref, taps_ref,
    layer_out, back_out, wpart_out, cpart_out,
    proj, halo_recv, pad, head, ahead_recv, cpad, pb, back_send, back_recv,
    h_ss, h_rs, a_ss, a_rs, b_ss, b_rs,
):
    n = lax.axis_size("seq")
    me = lax.axis_index("seq")
    rows, width = mixed_ref.shape
    groups = rows // 8
    edge = HALO // 8
    total = n * rows
    second = starts[0, 1]
    base = me * rows
    right, left = lax.rem(me + 1, n), lax.rem(me + n - 1, n)
    step = 256
    for t in range(width // step):
        cut = pl.ds(t * step, step)
        out = dot(mixed_ref[...], w_ref[:, cut]).astype(BF)
        proj[:, cut] = out
        pad[0, HALO : HALO + rows, cut] = out.astype(F32)
    greet(("seq",))
    halo = pltpu.make_async_remote_copy(
        src_ref=proj.at[pl.ds(rows - HALO, HALO)],
        dst_ref=halo_recv,
        send_sem=h_ss,
        recv_sem=h_rs,
        device_id={"seq": right},
    )
    halo.start()

    def frame(first, count):
        return lax.broadcasted_iota(jnp.int32, (count, width), 0) + first

    pad[1, HALO : HALO + rows, :] = jnp.where(
        frame(base, rows) >= second, pad[0, HALO : HALO + rows, :], 0.0
    )

    def later(g):
        return (base + 8 * g >= second).astype(jnp.int32)

    def conv_groups(which):
        def one_tile(t, _):
            cut = rows_at(t, 128)
            w = [jnp.broadcast_to(taps_ref[j : j + 1, cut], (8, 128)) for j in range(KERN)]
            for g in which:
                acc = jnp.zeros((8, 128), F32)
                lab = later(g)
                for j in range(KERN):
                    acc = acc + w[j] * pad[lab, 8 * g + j + 2 : 8 * g + j + 10, cut]
                gate = jax.nn.sigmoid(acc)
                here = slice(8 * g, 8 * g + 8)
                layer = pad[0, HALO + 8 * g : HALO + 8 * g + 8, cut] + acc * gate
                head[here, cut] = layer
                cot = cot_ref[here, cut].astype(F32)
                back = cot * (gate * (1.0 + acc * (1.0 - gate)))
                cpad[1, here, cut] = back
                cpad[0, here, cut] = jnp.where(base + 8 * g < second, back, 0.0)
            return 0

        lax.fori_loop(0, width // 128, one_tile, 0)

    conv_groups(range(edge, groups))
    halo.wait_recv()
    before = halo_recv[...].astype(F32)
    pad[0, 0:HALO, :] = jnp.where(me > 0, before, 0.0)
    pad[1, 0:HALO, :] = jnp.where(
        (frame(base - HALO, HALO) >= second) & (me > 0), before, 0.0
    )
    conv_groups(range(edge))
    pb[0:HALO, :] = cpad[1, 0:HALO, :].astype(BF)
    ahead = pltpu.make_async_remote_copy(
        src_ref=pb.at[pl.ds(0, HALO)],
        dst_ref=ahead_recv,
        send_sem=a_ss,
        recv_sem=a_rs,
        device_id={"seq": left},
    )
    ahead.start()
    layer_out[...] = head[...].astype(BF)

    def spread_groups(which):
        def one_tile(t, _):
            cut = rows_at(t, 128)
            w = [jnp.broadcast_to(taps_ref[j : j + 1, cut], (8, 128)) for j in range(KERN)]
            for g in which:
                acc = cot_ref[8 * g : 8 * g + 8, cut].astype(F32)
                lab = later(g)
                for j in range(KERN):
                    acc = acc + w[j] * cpad[lab, 8 * g + 30 - j : 8 * g + 38 - j, cut]
                head[8 * g : 8 * g + 8, cut] = acc
            return 0

        lax.fori_loop(0, width // 128, one_tile, 0)

    spread_groups(range(groups - edge))
    ahead.wait()
    after = ahead_recv[...].astype(F32)
    inside = me < n - 1
    cpad[1, rows : rows + HALO, :] = jnp.where(inside, after, 0.0)
    cpad[0, rows : rows + HALO, :] = jnp.where(
        (frame(base + rows, HALO) < second) & inside, after, 0.0
    )
    spread_groups(range(groups - edge, groups))
    pb[...] = head[...].astype(BF)
    for t in range(width // step):
        out = dot(pb[...], w_ref[t * step : (t + 1) * step, :], 1, 1).astype(BF).astype(F32)
        for u in range(step // 128):
            first, second_ = pack_halves(out[:, u * 128 : (u + 1) * 128])
            at = 2 * (t * (step // 128) + u)
            back_send[at] = first.astype(BF)
            back_send[at + 1] = second_.astype(BF)

    def back_copy(peer, owner, dst_dev):
        return pltpu.make_async_remote_copy(
            src_ref=back_send.at[peer],
            dst_ref=back_recv.at[owner],
            send_sem=b_ss.at[peer],
            recv_sem=b_rs.at[owner],
            device_id={"seq": dst_dev},
        )

    def start(d, _):
        peer = lax.rem(me + d, n)
        back_copy(peer, me, peer).start()
        return 0

    lax.fori_loop(1, n, start, 0)
    back_recv[me] = back_send[me]
    for t in range(width // step):
        cut = pl.ds(t * step, step)
        wpart_out[cut, :] = dot(mixed_ref[:, cut], pb[...], 0, 0).astype(BF)

    def tap_tile(t, _):
        cut = rows_at(t, 128)
        acc = [jnp.zeros((8, 128), F32)] * KERN
        for g in range(groups):
            lab = later(g)
            signal = cpad[1, 8 * g : 8 * g + 8, cut]
            for j in range(KERN):
                acc[j] = acc[j] + signal * pad[lab, 8 * g + j + 2 : 8 * g + j + 10, cut]
        for j in range(KERN):
            cpart_out[j : j + 1, cut] = jnp.sum(acc[j], axis=0, keepdims=True)
        cpart_out[KERN:, cut] = jnp.zeros((1, 128), F32)
        return 0

    lax.fori_loop(0, width // 128, tap_tile, 0)
    halo.wait_send()

    def settle(d, _):
        peer = lax.rem(me + d, n)
        back_copy(peer, me, peer).wait_send()
        back_copy(me, lax.rem(me - d + n, n), me).wait_recv()
        return 0

    lax.fori_loop(1, n, settle, 0)
    back_out[...] = back_recv[...]


def convolve(starts, mixed, weight, cot, taps):
    rows, width = mixed.shape
    n = lax.axis_size("seq")
    half = rows // 2
    shape = jax.ShapeDtypeStruct
    dma = pltpu.SemaphoreType.DMA
    return pl.pallas_call(
        conv_kernel,
        out_shape=[
            shape((rows, width), BF),
            shape((n, half, 128), BF),
            shape((width, width), BF),
            shape((KERN + 1, width), F32),
        ],
        in_specs=[SM, VM, VM, VM, VM],
        out_specs=[VM, VM, VM, VM],
        scratch_shapes=[
            pltpu.VMEM((rows, width), BF),
            pltpu.VMEM((HALO, width), BF),
            pltpu.VMEM((2, rows + HALO, width), F32),
            pltpu.VMEM((rows, width), F32),
            pltpu.VMEM((HALO, width), BF),
            pltpu.VMEM((2, rows + HALO, width), F32),
            pltpu.VMEM((rows, width), BF),
            pltpu.VMEM((n, half, 128), BF),
            pltpu.VMEM((n, half, 128), BF),
            dma, dma, dma, dma, dma((n,)), dma((n,)),
        ],
        compiler_params=pltpu.CompilerParams(
            collective_id=1, has_side_effects=True, vmem_limit_bytes=60 * 2**20
        ),
        name="convolve",
    )(starts, mixed, weight, cot, taps)


def bwd_kernel(
    p_hbm, kf_ref, qf_ref, kt_ref, aux_ref, back_ref,
    dq_out, dk_out, dv_out,
    of, qd, p_buf, dp, acc_k, acc_v, dqt, kv_send, kv_recv, q_send, q_recv,
    p_sem, kv_ss, kv_rs, q_ss, q_rs,
):
    n = lax.axis_size("seq")
    me = lax.axis_index("seq")
    rows, width = dq_out.shape
    half = rows // 2
    total = n * rows
    chunks = total // BLK
    group = SUB * BLK
    groups = total // group
    owners = group // rows
    first_group = me // (n // groups)

    def p_copy(i):
        g = lax.rem(first_group + i, groups)
        slot = lax.rem(i, 2)
        return pltpu.make_async_copy(
            p_hbm.at[:, rows_at(g, group), :], p_buf.at[slot], p_sem.at[slot]
        )

    p_copy(0).start()

    def prepare(p, _):
        x = back_ref[p].astype(F32)
        low = low_lanes(half)
        lane = lax.broadcasted_iota(jnp.int32, (half, 128), 1)
        for side in range(2):
            at = rows_at(2 * p + side, half)
            side_aux = aux_ref[at, :]
            inverse = jnp.where(low, side_aux, swap(side_aux))
            back = swap(x) if side == 0 else x
            back = jnp.where(low, 0.0, back * inverse).astype(BF)
            wide = back.astype(F32)
            delta = -jnp.sum(wide * side_aux, axis=1, keepdims=True)
            top = delta.astype(BF).astype(F32)
            mid = (delta - top).astype(BF).astype(F32)
            rest = delta - top - mid
            feat = jnp.where(
                lane == 2, top, jnp.where(lane == 3, mid, jnp.where(lane == 4, rest, 0.0))
            )
            of[at, 0:128] = back
            of[at, 128:256] = feat.astype(BF)
            qd[at, :] = (wide + qf_ref[at, 0:128].astype(F32)).astype(BF)
        return 0

    lax.fori_loop(0, n, prepare, 0)
    dqt[...] = jnp.zeros_like(dqt)
    greet(("seq",))

    def kv_copy(peer, owner, dst_dev):
        return pltpu.make_async_remote_copy(
            src_ref=kv_send.at[peer],
            dst_ref=kv_recv.at[owner],
            send_sem=kv_ss.at[peer],
            recv_sem=kv_rs.at[owner],
            device_id={"seq": dst_dev},
        )

    def q_copy(peer, owner, dst_dev):
        return pltpu.make_async_remote_copy(
            src_ref=q_send.at[peer],
            dst_ref=q_recv.at[owner],
            send_sem=q_ss.at[peer],
            recv_sem=q_rs.at[owner],
            device_id={"seq": dst_dev},
        )

    def one_group(i, _):
        g = lax.rem(first_group + i, groups)
        slot = lax.rem(i, 2)

        @pl.when(i + 1 < groups)
        def _():
            p_copy(i + 1).start()

        acc_k[...] = jnp.zeros_like(acc_k)
        acc_v[...] = jnp.zeros_like(acc_v)

        def prob_back(r, c):
            return dot(kf_ref[rows_at(g * SUB + r, BLK), :], of[rows_at(c, BLK), :], 1, 1)

        for r in range(SUB):
            dp[0, r * BLK : (r + 1) * BLK, :] = prob_back(r, 0)
        p_copy(i).wait()

        def two_chunks(pair, _):
            for par in range(2):
                c = 2 * pair + par
                ahead = lax.rem(c + 1, chunks)
                q_d = qd[rows_at(c, BLK), :]
                dq = jnp.zeros((HD, BLK), F32)
                for r in range(SUB):
                    cut = slice(r * BLK, (r + 1) * BLK)
                    dp[1 - par, cut, :] = prob_back(r, ahead)
                    p = p_buf[slot, c, cut, :]
                    ds = (p.astype(F32) * dp[par, cut, :]).astype(BF)
                    acc_v[cut, :] += dot(p, q_d)
                    acc_k[cut, :] += dot(ds, q_d)
                    dq = dq + dot(kt_ref[:, rows_at(g * SUB + r, BLK)], ds)
                dqt[:, rows_at(c, BLK)] += dq
            return 0

        lax.fori_loop(0, chunks // 2, two_chunks, 0)
        for w in range(owners):
            owner = g * owners + w
            cut = slice(w * rows, (w + 1) * rows)
            kv_send[owner] = jnp.where(low_lanes(rows), acc_k[cut, :], acc_v[cut, :]).astype(BF)

            @pl.when(owner != me)
            def _():
                kv_copy(owner, me, owner).start()

            @pl.when(owner == me)
            def _():
                kv_recv[owner] = kv_send[owner]

        return 0

    lax.fori_loop(0, groups, one_group, 0)
    aux = aux_ref
    for c in range(chunks):
        x = dqt[:, c * BLK : (c + 1) * BLK] * (HD**-0.5)
        acc_q = jnp.concatenate([x, jnp.zeros_like(x)], axis=0).T
        aux[c * BLK : (c + 1) * BLK, :] = acc_q

    def send_q(d, _):
        owner = lax.rem(me + d, n)
        top = aux[rows_at(2 * owner, half), :]
        bottom = aux[rows_at(2 * owner + 1, half), :]
        q_send[owner] = jnp.where(low_lanes(half), top, swap(bottom)).astype(BF)

        @pl.when(owner != me)
        def _():
            q_copy(owner, me, owner).start()

        @pl.when(owner == me)
        def _():
            q_recv[owner] = q_send[owner]

        return 0

    lax.fori_loop(1, n + 1, send_q, 0)

    def settle_kv(d, _):
        peer = lax.rem(me + d, n)
        kv_copy(peer, me, peer).wait_send()
        kv_copy(me, lax.rem(me - d + n, n), me).wait_recv()
        return 0

    lax.fori_loop(1, n, settle_kv, 0)
    low = low_lanes(rows)
    for t in range(width // 128):
        cut = slice(t * 128, (t + 1) * 128)
        one, two = kv_recv[2 * t].astype(F32), kv_recv[2 * t + 1].astype(F32)
        dk_out[:, cut] = jnp.where(low, one, swap(two)).astype(BF)
        dv_out[:, cut] = jnp.where(low, swap(one), two).astype(BF)

    def settle_q(d, _):
        peer = lax.rem(me + d, n)
        q_copy(peer, me, peer).wait_send()
        q_copy(me, lax.rem(me - d + n, n), me).wait_recv()
        return 0

    lax.fori_loop(1, n, settle_q, 0)
    for t in range(width // 128):
        cut = slice(t * 128, (t + 1) * 128)
        top, bottom = unpack_halves(q_recv[2 * t].astype(F32), q_recv[2 * t + 1].astype(F32))
        dq_out[0:half, cut] = top.astype(BF)
        dq_out[half:rows, cut] = bottom.astype(BF)


def backward(p, kf, qf, kt, aux, back, rows, width):
    n = lax.axis_size("seq")
    total = n * rows
    half = rows // 2
    shape = jax.ShapeDtypeStruct
    dma = pltpu.SemaphoreType.DMA

    def body(p_hbm, kf_ref, qf_ref, kt_ref, aux_in, back_ref, dq_out, dk_out, dv_out, aux, *rest):
        aux[...] = aux_in[...]
        bwd_kernel(p_hbm, kf_ref, qf_ref, kt_ref, aux, back_ref, dq_out, dk_out, dv_out, *rest)

    return pl.pallas_call(
        body,
        out_shape=[shape((rows, width), BF)] * 3,
        in_specs=[ANY, VM, VM, VM, VM, VM],
        out_specs=[VM, VM, VM],
        scratch_shapes=[
            pltpu.VMEM((total, 128), F32),
            pltpu.VMEM((total, 256), BF),
            pltpu.VMEM((total, 128), BF),
            pltpu.VMEM((2, total // BLK, SUB * BLK, BLK), BF),
            pltpu.VMEM((2, SUB * BLK, BLK), F32),
            pltpu.VMEM((SUB * BLK, 128), F32),
            pltpu.VMEM((SUB * BLK, 128), F32),
            pltpu.VMEM((HD, total), F32),
            pltpu.VMEM((n, rows, 128), BF),
            pltpu.VMEM((n, rows, 128), BF),
            pltpu.VMEM((n, half, 128), BF),
            pltpu.VMEM((n, half, 128), BF),
            dma((2,)), dma((n,)), dma((n,)), dma((n,)), dma((n,)),
        ],
        compiler_params=pltpu.CompilerParams(
            collective_id=2, has_side_effects=True, vmem_limit_bytes=60 * 2**20
        ),
        name="attend_back",
    )(p, kf, qf, kt, aux, back)


def reduce_kernel(
    factor, w_ref, out_ref, one, sums, two, mine, three, part, four, five,
    s1, r1, s2, r2, s3, r3, s4, r4, s5, r5, s6, r6,
):
    n, groups = lax.axis_size("seq"), lax.axis_size("dp")
    me, dp = lax.axis_index("seq"), lax.axis_index("dp")
    width = w_ref.shape[0]
    core, z = lax.rem(me, 2), me // 2
    deep = n // 2
    half = width // 2
    blk = half // groups
    lanes = width // deep
    sibling = me + 1 - 2 * core
    greet(("seq", "dp"))
    c1 = pltpu.make_async_remote_copy(
        src_ref=w_ref.at[rows_at(1 - core, half), :],
        dst_ref=one,
        send_sem=s1,
        recv_sem=r1,
        device_id={"seq": sibling},
    )
    c1.start()
    c1.wait_recv()

    def add(i, _):
        cut = rows_at(i, blk)
        own = w_ref[pl.ds(pl.multiple_of(core * half + i * blk, blk), blk), :]
        sums[cut, :] = (own.astype(F32) + one[cut, :].astype(F32)).astype(BF)
        return 0

    lax.fori_loop(0, groups, add, 0)

    def c2(peer, owner, dev):
        return pltpu.make_async_remote_copy(
            src_ref=sums.at[rows_at(peer, blk), :],
            dst_ref=two.at[owner],
            send_sem=s2.at[peer],
            recv_sem=r2.at[owner],
            device_id={"dp": dev},
        )

    def start2(d, _):
        peer = lax.rem(dp + d, groups)
        c2(peer, dp, peer).start()
        return 0

    lax.fori_loop(1, groups, start2, 0)

    def take2(d, total):
        src = lax.rem(dp - d + groups, groups)
        c2(dp, src, dp).wait_recv()
        return total + two[src].astype(F32)

    total = lax.fori_loop(1, groups, take2, sums[rows_at(dp, blk), :].astype(F32))
    mine[...] = total.astype(BF)

    def at_z(index):
        return index * 2 + core

    def c3(peer, owner, dev):
        return pltpu.make_async_remote_copy(
            src_ref=mine.at[:, rows_at(peer, lanes)],
            dst_ref=three.at[owner],
            send_sem=s3.at[peer],
            recv_sem=r3.at[owner],
            device_id={"seq": at_z(dev)},
        )

    def start3(d, _):
        peer = lax.rem(z + d, deep)
        c3(peer, z, peer).start()
        return 0

    lax.fori_loop(1, deep, start3, 0)

    def take3(d, total):
        src = lax.rem(z - d + deep, deep)
        c3(z, src, z).wait_recv()
        return total + three[src].astype(F32)

    total = lax.fori_loop(1, deep, take3, mine[:, rows_at(z, lanes)].astype(F32))
    part[...] = total.astype(BF)
    four[:, rows_at(z, lanes)] = part[...]

    def c4(peer, owner, dev):
        return pltpu.make_async_remote_copy(
            src_ref=part,
            dst_ref=four.at[:, rows_at(owner, lanes)],
            send_sem=s4.at[peer],
            recv_sem=r4.at[owner],
            device_id={"seq": at_z(dev)},
        )

    def start4(d, _):
        peer = lax.rem(z + d, deep)
        c4(peer, z, peer).start()
        return 0

    lax.fori_loop(1, deep, start4, 0)

    def take4(d, _):
        c4(z, lax.rem(z - d + deep, deep), z).wait_recv()
        return 0

    lax.fori_loop(1, deep, take4, 0)
    five[rows_at(core * groups + dp, blk), :] = four[...]

    def c5(peer, owner, dev):
        return pltpu.make_async_remote_copy(
            src_ref=four,
            dst_ref=five.at[rows_at(core * groups + owner, blk), :],
            send_sem=s5.at[peer],
            recv_sem=r5.at[owner],
            device_id={"dp": dev},
        )

    def start5(d, _):
        peer = lax.rem(dp + d, groups)
        c5(peer, dp, peer).start()
        return 0

    lax.fori_loop(1, groups, start5, 0)

    def take5(d, _):
        c5(dp, lax.rem(dp - d + groups, groups), dp).wait_recv()
        return 0

    lax.fori_loop(1, groups, take5, 0)

    def c6(owner):
        return pltpu.make_async_remote_copy(
            src_ref=five.at[rows_at(owner, half), :],
            dst_ref=five.at[rows_at(owner, half), :],
            send_sem=s6,
            recv_sem=r6,
            device_id={"seq": sibling},
        )

    c6(core).start()
    c6(1 - core).wait_recv()
    for i in range(width // BLK):
        cut = pl.ds(i * BLK, BLK)
        out_ref[cut, :] = five[cut, :].astype(F32) * factor
    c1.wait_send()
    c6(core).wait_send()

    def settle_dp(d, _):
        peer = lax.rem(dp + d, groups)
        c2(peer, dp, peer).wait_send()
        c5(peer, dp, peer).wait_send()
        return 0

    lax.fori_loop(1, groups, settle_dp, 0)

    def settle_z(d, _):
        peer = lax.rem(z + d, deep)
        c3(peer, z, peer).wait_send()
        c4(peer, z, peer).wait_send()
        return 0

    lax.fori_loop(1, deep, settle_z, 0)


def reduce_weight(part, factor):
    width = part.shape[0]
    n, groups = lax.axis_size("seq"), lax.axis_size("dp")
    half, deep = width // 2, n // 2
    blk, lanes = half // groups, width // deep
    dma = pltpu.SemaphoreType.DMA
    return pl.pallas_call(
        functools.partial(reduce_kernel, factor),
        out_shape=jax.ShapeDtypeStruct((width, width), F32),
        in_specs=[VM],
        out_specs=VM,
        scratch_shapes=[
            pltpu.VMEM((half, width), BF),
            pltpu.VMEM((half, width), BF),
            pltpu.VMEM((groups, blk, width), BF),
            pltpu.VMEM((blk, width), BF),
            pltpu.VMEM((deep, blk, lanes), BF),
            pltpu.VMEM((blk, lanes), BF),
            pltpu.VMEM((blk, width), BF),
            pltpu.VMEM((width, width), BF),
            dma, dma, dma((groups,)), dma((groups,)), dma((deep,)), dma((deep,)),
            dma((deep,)), dma((deep,)), dma((groups,)), dma((groups,)), dma, dma,
        ],
        compiler_params=pltpu.CompilerParams(
            collective_id=3, has_side_effects=True, vmem_limit_bytes=40 * 2**20
        ),
        name="reduce_weight",
    )(part)


def local(query_proj, key_proj, value_proj, cotangent, out_weight, conv_weight, rec_starts):
    rows, width = query_proj.shape[1:]
    factor = (lax.axis_size("dp") * lax.axis_size("seq") * rows) ** -0.5
    p, kf, qf, kt, aux, mixed = forward(rec_starts, query_proj[0], key_proj[0], value_proj[0])
    layer, back, weight_part, conv_part = convolve(
        rec_starts, mixed, out_weight, cotangent[0], conv_weight
    )
    conv_grad = lax.psum(conv_part[:KERN], ("dp", "seq")) * factor
    weight_grad = reduce_weight(weight_part, factor)
    dq, dk, dv = backward(p, kf, qf, kt, aux, back, rows, width)
    return layer[None], dq[None], dk[None], dv[None], weight_grad, conv_grad


def solution(mesh):
    frames = P("dp", "seq", None)
    return jax.shard_map(
        local,
        mesh=mesh,
        in_specs=(frames, frames, frames, frames, P(), P(), P("dp", None)),
        out_specs=(frames, frames, frames, frames, P(), P()),
        check_vma=False,
    )
```

time: 615 us -> 366 us (0.60)
  Pallas kernels: 0 us -> 197 us
  waiting for transfers between devices: 315 us -> 143 us
  matrix products: 84.2 us -> 0 us
  other arithmetic: 76 us -> 1.57 us
  local copies, waits for them, and re-layouts: 68.6 us -> 9.73 us
  starting transfers between devices: 42.8 us -> 0.04 us
  loops' own time: 8.71 us -> 0 us
    pallas_call x0 -> x4, Pallas kernels: none -> 197 us  [the longest x1 59.9 us: forward(): pl.pallas_call(fwd_kernel, out_shape=[shape((total // BLK, total, BLK), B...]
    all_to_all x8 -> x0, waiting for transfers between devices: 89.7 us -> none  [the longest x1 15.2 us: local(): lax.all_to_all(key_proj[0], 'seq', split_axis=1, concat_axis=0, tiled=True)]
    dot_general x45 -> x0, matrix products: 84.2 us -> none  [the longest x12 28.9 us: block_scores(): jnp.einsum('qhd,khd->hqk', query_blk, key_part, preferred_element_type=jn...]
    psum x1, waiting for transfers between devices: 226 us -> 143 us  [local(): conv_grad = lax.psum(conv_part[:KERN], ('dp', 'seq')) * factor]
    reduce_sum x21 -> x0, other arithmetic: 52 us -> none  [the longest x6 38.3 us: tap_sums(): rows_out.append(jnp.sum(jnp.where(same, signal * window, 0.0), axis=0))]
    all_to_all x8 -> x0, starting transfers between devices: 38.2 us -> none  [the longest x1 9.98 us: local(): lax.all_to_all(query_proj[0], 'seq', split_axis=1, concat_axis=0, tiled=T...]
    all_to_all x12 -> x0, local copies, waits for them, and re-layouts: 17.3 us -> none  [the longest x2 4.47 us: local(): lax.all_to_all(mixed_heads.reshape(total, -1), 'seq', split_axis=0, conca...]
    dynamic_slice x30 -> x0, local copies, waits for them, and re-layouts: 12.4 us -> none  [the longest x12 7.44 us: forward_dense(): lax.map(forward_one_block, jnp.arange(count, dtype=jnp.int32))]
  transfers between devices with their start and end apart: 11 -> 1, of which waited for: 9 -> 1; matrix products, arithmetic and copies ran while one was open for 9% -> 0% of each run, Pallas kernels for 0% -> 29%
where the time goes in v1:
time: 366 us
  Pallas kernels  197 us (54%)
  waiting for transfers between devices  143 us (39%)
  between operations  14.1 us (4%)
  local copies, waits for them, and re-layouts  9.73 us (3%)
    psum x1, waiting for transfers between devices, local(): conv_grad = lax.psum(conv_part[:KERN], ('dp', 'seq')) * factor  143 us
    pallas_call x1, Pallas kernels, forward(): pl.pallas_call(fwd_kernel, out_shape=[shape((total // BLK, total, BLK), B...  59.9 us
    pallas_call x1, Pallas kernels, backward(): pl.pallas_call(body, out_shape=[shape((rows, width), BF)] * 3, in_specs=[...  56.3 us
    pallas_call x1, Pallas kernels, reduce_weight(): pl.pallas_call(functools.partial(reduce_kernel, factor), out_shape=jax.Sh...  50.4 us
    pallas_call x1, Pallas kernels, convolve(): pl.pallas_call(conv_kernel, out_shape=[shape((rows, width), BF), shape((n...  30.8 us
    unnamed x17, local copies, waits for them, and re-layouts  9.73 us
  transfers between devices with their start and end apart: 1, of which 1 were waited for; matrix products, arithmetic and copies ran while one was open for 0% of the time, Pallas kernels for 29%

profile of v1, /device:TPU:1, one launch (start us, length us, event | category | flops | bytes accessed | tf_op | source)
XLA Modules:
  0.0 365.8 jit_solution(2658676712643660348)
XLA Ops:
  7.2 0.0 all-reduce.2.cloned.1.call-start
  7.2 59.9 %attend.1 = (bf16[12,3072,256]{2,1,0:T(8,128)(2,1)}, bf16[3072,256]{1,0:T(8,128)(2,1)}, bf16[3072,256]{1,0:T(8,128)(2,1)}, bf16[64,3072]{1,0:T(8,128)(2,1)}, f32...) custom-call(s32[1,2]{1,0:T(1,128)} %starts.3, bf16[192,1024]{1,0:T(8,128)(2,1)} %bitcast.14, bf16[192,1024]{1,0:T(8,128)(2,1)} %bitcast.15, ...), custom_call_target="tpu_custom_call" | custom-call | tf_op jit(solution)/shard_map/attend/pallas_call | solution.py:268
  67.1 30.8 %convolve.1 = (bf16[192,1024]{1,0:T(8,128)(2,1)}, bf16[16,96,128]{2,1,0:T(8,128)(2,1)}, bf16[1024,1024]{1,0:T(8,128)(2,1)}, f32[32,1024]{1,0:T(8,128)}) custom-call(s32[1,2]{1,0:T(1,128)} %starts.3, bf16[192,1024]{1,0:T(8,128)(2,1)} %get-tuple-element.19.mixed_ref, bf16[1024,1024]{1,0:T(8,128)(2,1)} %w_ref.1, bf16[192,1024]{1,0:T(8,128)(2,1)} %bitcast.9, ...), custom_call_target="tpu_custom_call" | custom-call | tf_op jit(solution)/shard_map/convolve/pallas_call | solution.py:468
  98.0 0.0 all-reduce.2.cloned.1.call-update
  98.0 0.0 copy-start.1
  98.0 56.3 %attend_back.1 = (bf16[192,1024]{1,0:T(8,128)(2,1)}, bf16[192,1024]{1,0:T(8,128)(2,1)}, bf16[192,1024]{1,0:T(8,128)(2,1)}) custom-call(bf16[12,3072,256]{2,1,0:T(8,128)(2,1)} %get-tuple-element.21.p_hbm, bf16[3072,256]{1,0:T(8,128)(2,1)} %get-tuple-element.22.kf_ref, bf16[3072,256]{1,0:T(8,128)(2,1)} %get-tuple-element.23.qf_ref, ...), custom_call_target="tpu_custom_call" | custom-call | tf_op jit(solution)/shard_map/attend_back/pallas_call | solution.py:683
  154.3 0.0 copy-done.1
  154.3 0.0 copy-start.2
  154.3 0.0 copy-start.5
  154.3 50.4 %reduce_weight.1 = f32[1024,1024]{1,0:T(8,128)S(1)} custom-call(bf16[1024,1024]{1,0:T(8,128)(2,1)S(1)} %copy-done.1), custom_call_target="tpu_custom_call" | custom-call | tf_op jit(solution)/shard_map/reduce_weight/pallas_call | solution.py:879
  204.7 0.0 copy-start
  204.7 1.9 copy-done
  206.7 0.0 copy-start.4
  206.7 0.0 copy-start.3
  206.7 142.9 %all-reduce.2.cloned.1.call-done = f32[31,1024]{1,0:T(8,128)} async-done(((f32[31,1024]{1,0:T(8,128)}), f32[31,1024]{1,0:T(8,128)}) %all-reduce.2.cloned.1.call-update) | async-done | bytes 126992 | tf_op jit(solution)/shard_map/psum | solution.py:910
  349.6 1.6 broadcast_multiply_fusion
  351.2 0.0 copy-done.2
  351.2 0.7 copy.19
  351.9 0.0 copy-done.5
  351.9 0.7 copy.20
  352.7 0.0 copy-done.4
  352.7 0.7 copy.21
  353.4 0.0 copy-done.3
  353.4 0.7 copy.22
  354.2 4.8 %copy.23 = f32[1024,1024]{1,0:T(8,128)} copy(f32[1024,1024]{1,0:T(8,128)} %copy-done) | data formatting | bytes 8388608
Async XLA Ops:
  7.2 342.4 %all-reduce.2.cloned.1.call-start = ((), (), s32[]{:S(2)}) async-start(), calls=%async_computation | async-start | bytes 262144 | tf_op jit(solution)/shard_map/psum | solution.py:910
  98.0 56.3 %copy-start.1 = (bf16[1024,1024]{1,0:T(8,128)(2,1)S(1)}, bf16[1024,1024]{1,0:T(8,128)(2,1)}, u32[]{:S(2)}) copy-start(bf16[1024,1024]{1,0:T(8,128)(2,1)} %get-tuple-element.30.w_ref) | copy-start | bytes 6291460
  154.3 196.9 %copy-start.2 = (bf16[192,1024]{1,0:T(8,128)(2,1)S(1)}, bf16[192,1024]{1,0:T(8,128)(2,1)}, u32[]{:S(2)}) copy-start(bf16[192,1024]{1,0:T(8,128)(2,1)} %get-tuple-element.20) | copy-start | bytes 1179652
  154.3 197.6 %copy-start.5 = (bf16[192,1024]{1,0:T(8,128)(2,1)S(1)}, bf16[192,1024]{1,0:T(8,128)(2,1)}, u32[]{:S(2)}) copy-start(bf16[192,1024]{1,0:T(8,128)(2,1)} %get-tuple-element.27) | copy-start | bytes 1179652
  204.7 1.9 copy-start
  206.7 146.0 %copy-start.4 = (bf16[192,1024]{1,0:T(8,128)(2,1)S(1)}, bf16[192,1024]{1,0:T(8,128)(2,1)}, u32[]{:S(2)}) copy-start(bf16[192,1024]{1,0:T(8,128)(2,1)} %get-tuple-element.28) | copy-start | bytes 1179652
  206.7 146.7 %copy-start.3 = (bf16[192,1024]{1,0:T(8,128)(2,1)S(1)}, bf16[192,1024]{1,0:T(8,128)(2,1)}, u32[]{:S(2)}) copy-start(bf16[192,1024]{1,0:T(8,128)(2,1)} %get-tuple-element.29) | copy-start | bytes 1179652
Sparse Core Ops, SparseCore 0:
  98.1 251.4 all-reduce.1

commit v2 on v1

--- a/solution.py
+++ b/solution.py
@@ -495,14 +495,15 @@
 
 
 def bwd_kernel(
-    p_hbm, kf_ref, qf_ref, kt_ref, aux_ref, back_ref,
-    dq_out, dk_out, dv_out,
+    p_hbm, kf_ref, qf_ref, kt_ref, aux_ref, back_ref, w_ref, conv_ref,
+    dq_out, dk_out, dv_out, w_out, conv_out,
     of, qd, p_buf, dp, acc_k, acc_v, dqt, kv_send, kv_recv, q_send, q_recv,
-    p_sem, kv_ss, kv_rs, q_ss, q_rs,
+    p_sem, kv_ss, kv_rs, q_ss, q_rs, *reduce_refs,
 ):
     n = lax.axis_size("seq")
     me = lax.axis_index("seq")
     rows, width = dq_out.shape
+    steps = reducer(w_ref, conv_ref, w_out, conv_out, reduce_refs[:12], reduce_refs[12:])
     half = rows // 2
     total = n * rows
     chunks = total // BLK
@@ -545,7 +546,9 @@
 
     lax.fori_loop(0, n, prepare, 0)
     dqt[...] = jnp.zeros_like(dqt)
-    greet(("seq",))
+    greet(("seq", "dp"))
+    steps[0]()
+    places = {0: 1, 2: 2, 3: 3, 4: 4, 6: 5} if groups >= 4 else {0: 1, 1: 2, 2: 3, 3: 4}
 
     def kv_copy(peer, owner, dst_dev):
         return pltpu.make_async_remote_copy(
@@ -600,7 +603,11 @@
                 dqt[:, rows_at(c, BLK)] += dq
             return 0
 
-        lax.fori_loop(0, chunks // 2, two_chunks, 0)
+        for h in range(2):
+            lax.fori_loop(h * chunks // 4, (h + 1) * chunks // 4, two_chunks, 0)
+            for place, number in places.items():
+                if place % 2 == h:
+                    pl.when(i == place // 2)(steps[number])
         for w in range(owners):
             owner = g * owners + w
             cut = slice(w * rows, (w + 1) * rows)
@@ -640,6 +647,8 @@
         return 0
 
     lax.fori_loop(1, n + 1, send_q, 0)
+    if 5 not in places.values():
+        steps[5]()
 
     def settle_kv(d, _):
         peer = lax.rem(me + d, n)
@@ -648,6 +657,7 @@
         return 0
 
     lax.fori_loop(1, n, settle_kv, 0)
+    steps[6]()
     low = low_lanes(rows)
     for t in range(width // 128):
         cut = slice(t * 128, (t + 1) * 128)
@@ -669,22 +679,27 @@
         dq_out[half:rows, cut] = bottom.astype(BF)
 
 
-def backward(p, kf, qf, kt, aux, back, rows, width):
-    n = lax.axis_size("seq")
+def backward(p, kf, qf, kt, aux, back, w_part, conv_part, rows):
+    n, groups = lax.axis_size("seq"), lax.axis_size("dp")
+    width = w_part.shape[0]
+    bufs, sems = reducer_bufs(width, n, groups)
     total = n * rows
     half = rows // 2
     shape = jax.ShapeDtypeStruct
     dma = pltpu.SemaphoreType.DMA
 
-    def body(p_hbm, kf_ref, qf_ref, kt_ref, aux_in, back_ref, dq_out, dk_out, dv_out, aux, *rest):
+    def body(p_hbm, kf_ref, qf_ref, kt_ref, aux_in, *rest):
+        outs = rest[3:8]
+        aux = rest[8]
         aux[...] = aux_in[...]
-        bwd_kernel(p_hbm, kf_ref, qf_ref, kt_ref, aux, back_ref, dq_out, dk_out, dv_out, *rest)
+        bwd_kernel(p_hbm, kf_ref, qf_ref, kt_ref, aux, *rest[:3], *outs, *rest[9:])
 
     return pl.pallas_call(
         body,
-        out_shape=[shape((rows, width), BF)] * 3,
-        in_specs=[ANY, VM, VM, VM, VM, VM],
-        out_specs=[VM, VM, VM],
+        out_shape=[shape((rows, width), BF)] * 3
+        + [shape((width, width), BF), shape((KERN + 1, width), F32)],
+        in_specs=[ANY] + [VM] * 7,
+        out_specs=[VM] * 5,
         scratch_shapes=[
             pltpu.VMEM((total, 128), F32),
             pltpu.VMEM((total, 256), BF),
@@ -699,18 +714,18 @@
             pltpu.VMEM((n, half, 128), BF),
             pltpu.VMEM((n, half, 128), BF),
             dma((2,)), dma((n,)), dma((n,)), dma((n,)), dma((n,)),
+            *bufs, *sems,
         ],
         compiler_params=pltpu.CompilerParams(
             collective_id=2, has_side_effects=True, vmem_limit_bytes=60 * 2**20
         ),
         name="attend_back",
-    )(p, kf, qf, kt, aux, back)
-
-
-def reduce_kernel(
-    factor, w_ref, out_ref, one, sums, two, mine, three, part, four, five,
-    s1, r1, s2, r2, s3, r3, s4, r4, s5, r5, s6, r6,
-):
+    )(p, kf, qf, kt, aux, back, w_part, conv_part)
+
+
+def reducer(w_ref, conv_ref, w_out, conv_out, bufs, sems):
+    one, sums, two, mine, three, part, four, conv_one, conv_sums, conv_two, conv_three, conv_part = bufs
+    s1, r1, s2, r2, s3, r3, s4, r4, s5, r5, s6, r6 = sems
     n, groups = lax.axis_size("seq"), lax.axis_size("dp")
     me, dp = lax.axis_index("seq"), lax.axis_index("dp")
     width = w_ref.shape[0]
@@ -719,185 +734,184 @@
     half = width // 2
     blk = half // groups
     lanes = width // deep
+    conv_half = (KERN + 1) // 2
+    per_row = groups // 2
+    conv_lanes = width // per_row
     sibling = me + 1 - 2 * core
-    greet(("seq", "dp"))
-    c1 = pltpu.make_async_remote_copy(
-        src_ref=w_ref.at[rows_at(1 - core, half), :],
-        dst_ref=one,
-        send_sem=s1,
-        recv_sem=r1,
-        device_id={"seq": sibling},
-    )
-    c1.start()
-    c1.wait_recv()
-
-    def add(i, _):
-        cut = rows_at(i, blk)
-        own = w_ref[pl.ds(pl.multiple_of(core * half + i * blk, blk), blk), :]
-        sums[cut, :] = (own.astype(F32) + one[cut, :].astype(F32)).astype(BF)
-        return 0
-
-    lax.fori_loop(0, groups, add, 0)
+
+    def send(src, dst, ss, rs, dev):
+        return pltpu.make_async_remote_copy(
+            src_ref=src, dst_ref=dst, send_sem=ss, recv_sem=rs, device_id=dev
+        )
+
+    def tile(ref, index, first=0):
+        row = pl.multiple_of(first + 8 * (index // per_row), 8)
+        return ref.at[pl.ds(row, 8), rows_at(lax.rem(index, per_row), conv_lanes)]
+
+    def c1():
+        dev = {"seq": sibling}
+        return (
+            send(w_ref.at[rows_at(1 - core, half), :], one, s1.at[0], r1.at[0], dev),
+            send(conv_ref.at[rows_at(1 - core, conv_half), :], conv_one, s1.at[1], r1.at[1], dev),
+        )
 
     def c2(peer, owner, dev):
-        return pltpu.make_async_remote_copy(
-            src_ref=sums.at[rows_at(peer, blk), :],
-            dst_ref=two.at[owner],
-            send_sem=s2.at[peer],
-            recv_sem=r2.at[owner],
-            device_id={"dp": dev},
-        )
-
-    def start2(d, _):
-        peer = lax.rem(dp + d, groups)
-        c2(peer, dp, peer).start()
-        return 0
-
-    lax.fori_loop(1, groups, start2, 0)
-
-    def take2(d, total):
-        src = lax.rem(dp - d + groups, groups)
-        c2(dp, src, dp).wait_recv()
-        return total + two[src].astype(F32)
-
-    total = lax.fori_loop(1, groups, take2, sums[rows_at(dp, blk), :].astype(F32))
-    mine[...] = total.astype(BF)
-
-    def at_z(index):
-        return index * 2 + core
+        dev = {"dp": dev}
+        return (
+            send(sums.at[rows_at(peer, blk), :], two.at[owner], s2.at[0, peer], r2.at[0, owner], dev),
+            send(tile(conv_sums, peer), conv_two.at[owner], s2.at[1, peer], r2.at[1, owner], dev),
+        )
 
     def c3(peer, owner, dev):
-        return pltpu.make_async_remote_copy(
-            src_ref=mine.at[:, rows_at(peer, lanes)],
-            dst_ref=three.at[owner],
-            send_sem=s3.at[peer],
-            recv_sem=r3.at[owner],
-            device_id={"seq": at_z(dev)},
-        )
-
-    def start3(d, _):
-        peer = lax.rem(z + d, deep)
-        c3(peer, z, peer).start()
-        return 0
-
-    lax.fori_loop(1, deep, start3, 0)
-
-    def take3(d, total):
-        src = lax.rem(z - d + deep, deep)
-        c3(z, src, z).wait_recv()
-        return total + three[src].astype(F32)
-
-    total = lax.fori_loop(1, deep, take3, mine[:, rows_at(z, lanes)].astype(F32))
-    part[...] = total.astype(BF)
-    four[:, rows_at(z, lanes)] = part[...]
+        dev = {"seq": dev * 2 + core}
+        return (
+            send(mine.at[:, rows_at(peer, lanes)], three.at[owner], s3.at[0, peer], r3.at[0, owner], dev),
+            send(conv_part, conv_three.at[owner], s3.at[1, peer], r3.at[1, owner], dev),
+        )
 
     def c4(peer, owner, dev):
-        return pltpu.make_async_remote_copy(
-            src_ref=part,
-            dst_ref=four.at[:, rows_at(owner, lanes)],
-            send_sem=s4.at[peer],
-            recv_sem=r4.at[owner],
-            device_id={"seq": at_z(dev)},
-        )
-
-    def start4(d, _):
-        peer = lax.rem(z + d, deep)
-        c4(peer, z, peer).start()
-        return 0
-
-    lax.fori_loop(1, deep, start4, 0)
-
-    def take4(d, _):
-        c4(z, lax.rem(z - d + deep, deep), z).wait_recv()
-        return 0
-
-    lax.fori_loop(1, deep, take4, 0)
-    five[rows_at(core * groups + dp, blk), :] = four[...]
+        dev = {"seq": dev * 2 + core}
+        return (send(part, four.at[:, rows_at(owner, lanes)], s4.at[peer], r4.at[owner], dev),)
 
     def c5(peer, owner, dev):
-        return pltpu.make_async_remote_copy(
-            src_ref=four,
-            dst_ref=five.at[rows_at(core * groups + owner, blk), :],
-            send_sem=s5.at[peer],
-            recv_sem=r5.at[owner],
-            device_id={"dp": dev},
-        )
-
-    def start5(d, _):
-        peer = lax.rem(dp + d, groups)
-        c5(peer, dp, peer).start()
-        return 0
-
-    lax.fori_loop(1, groups, start5, 0)
-
-    def take5(d, _):
-        c5(dp, lax.rem(dp - d + groups, groups), dp).wait_recv()
-        return 0
-
-    lax.fori_loop(1, groups, take5, 0)
+        dev = {"dp": dev}
+        to = w_out.at[rows_at(core * groups + owner, blk), :]
+        return (
+            send(four, to, s5.at[0, peer], r5.at[0, owner], dev),
+            send(conv_part, tile(conv_out, owner, core * conv_half), s5.at[1, peer], r5.at[1, owner], dev),
+        )
 
     def c6(owner):
-        return pltpu.make_async_remote_copy(
-            src_ref=five.at[rows_at(owner, half), :],
-            dst_ref=five.at[rows_at(owner, half), :],
-            send_sem=s6,
-            recv_sem=r6,
-            device_id={"seq": sibling},
-        )
-
-    c6(core).start()
-    c6(1 - core).wait_recv()
-    for i in range(width // BLK):
-        cut = pl.ds(i * BLK, BLK)
-        out_ref[cut, :] = five[cut, :].astype(F32) * factor
-    c1.wait_send()
-    c6(core).wait_send()
-
-    def settle_dp(d, _):
-        peer = lax.rem(dp + d, groups)
-        c2(peer, dp, peer).wait_send()
-        c5(peer, dp, peer).wait_send()
-        return 0
-
-    lax.fori_loop(1, groups, settle_dp, 0)
-
-    def settle_z(d, _):
-        peer = lax.rem(z + d, deep)
-        c3(peer, z, peer).wait_send()
-        c4(peer, z, peer).wait_send()
-        return 0
-
-    lax.fori_loop(1, deep, settle_z, 0)
-
-
-def reduce_weight(part, factor):
-    width = part.shape[0]
-    n, groups = lax.axis_size("seq"), lax.axis_size("dp")
+        dev = {"seq": sibling}
+        here, there = w_out.at[rows_at(owner, half), :], conv_out.at[rows_at(owner, conv_half), :]
+        return send(here, here, s6.at[0], r6.at[0], dev), send(there, there, s6.at[1], r6.at[1], dev)
+
+    def to_all(copies, own, count):
+        def go(d, _):
+            peer = lax.rem(own + d, count)
+            for copy in copies(peer, own, peer):
+                copy.start()
+            return 0
+
+        lax.fori_loop(1, count, go, 0)
+
+    def from_all(copies, own, count):
+        def go(d, _):
+            for copy in copies(own, lax.rem(own - d + count, count), own):
+                copy.wait_recv()
+            return 0
+
+        lax.fori_loop(1, count, go, 0)
+
+    def step0():
+        for copy in c1():
+            copy.start()
+
+    def step1():
+        for copy in c1():
+            copy.wait_recv()
+
+        def add(i, _):
+            cut = rows_at(i, blk)
+            own = w_ref[pl.ds(pl.multiple_of(core * half + i * blk, blk), blk), :]
+            sums[cut, :] = (own.astype(F32) + one[cut, :].astype(F32)).astype(BF)
+            return 0
+
+        lax.fori_loop(0, groups, add, 0)
+        conv_sums[...] = conv_ref[rows_at(core, conv_half), :] + conv_one[...]
+        to_all(c2, dp, groups)
+
+    def step2():
+        from_all(c2, dp, groups)
+        two[dp] = sums[rows_at(dp, blk), :]
+        conv_two[dp] = tile(conv_sums, dp)[...]
+
+        def add(i, total):
+            return total[0] + two[i].astype(F32), total[1] + conv_two[i]
+
+        zero = jnp.zeros((blk, width), F32), jnp.zeros((8, conv_lanes), F32)
+        total = lax.fori_loop(0, groups, add, zero)
+        mine[...] = total[0].astype(BF)
+        conv_part[...] = total[1]
+        to_all(c3, z, deep)
+
+    def step3():
+        from_all(c3, z, deep)
+        three[z] = mine[:, rows_at(z, lanes)]
+        conv_three[z] = conv_part[...]
+        total, conv_total = jnp.zeros((blk, lanes), F32), jnp.zeros((8, conv_lanes), F32)
+        for i in range(deep):
+            total = total + three[i].astype(F32)
+            conv_total = conv_total + conv_three[i]
+        part[...] = total.astype(BF)
+        four[:, rows_at(z, lanes)] = part[...]
+
+        def settle(d, _):
+            c3(lax.rem(z + d, deep), z, lax.rem(z + d, deep))[1].wait_send()
+            return 0
+
+        lax.fori_loop(1, deep, settle, 0)
+        conv_part[...] = conv_total
+        to_all(c4, z, deep)
+
+    def step4():
+        from_all(c4, z, deep)
+        w_out[rows_at(core * groups + dp, blk), :] = four[...]
+        tile(conv_out, dp, core * conv_half)[...] = conv_part[...]
+        to_all(c5, dp, groups)
+
+    def step5():
+        from_all(c5, dp, groups)
+        for copy in c6(core):
+            copy.start()
+
+    def step6():
+        for copy in c6(1 - core):
+            copy.wait_recv()
+        for copy in (*c1(), *c6(core)):
+            copy.wait_send()
+
+        def settle_dp(d, _):
+            peer = lax.rem(dp + d, groups)
+            for copy in (*c2(peer, dp, peer), *c5(peer, dp, peer)):
+                copy.wait_send()
+            return 0
+
+        lax.fori_loop(1, groups, settle_dp, 0)
+
+        def settle_z(d, _):
+            peer = lax.rem(z + d, deep)
+            for copy in (c3(peer, z, peer)[0], *c4(peer, z, peer)):
+                copy.wait_send()
+            return 0
+
+        lax.fori_loop(1, deep, settle_z, 0)
+
+    return step0, step1, step2, step3, step4, step5, step6
+
+
+def reducer_bufs(width, n, groups):
     half, deep = width // 2, n // 2
     blk, lanes = half // groups, width // deep
+    conv_half, conv_lanes = (KERN + 1) // 2, width // (groups // 2)
     dma = pltpu.SemaphoreType.DMA
-    return pl.pallas_call(
-        functools.partial(reduce_kernel, factor),
-        out_shape=jax.ShapeDtypeStruct((width, width), F32),
-        in_specs=[VM],
-        out_specs=VM,
-        scratch_shapes=[
-            pltpu.VMEM((half, width), BF),
-            pltpu.VMEM((half, width), BF),
-            pltpu.VMEM((groups, blk, width), BF),
-            pltpu.VMEM((blk, width), BF),
-            pltpu.VMEM((deep, blk, lanes), BF),
-            pltpu.VMEM((blk, lanes), BF),
-            pltpu.VMEM((blk, width), BF),
-            pltpu.VMEM((width, width), BF),
-            dma, dma, dma((groups,)), dma((groups,)), dma((deep,)), dma((deep,)),
-            dma((deep,)), dma((deep,)), dma((groups,)), dma((groups,)), dma, dma,
-        ],
-        compiler_params=pltpu.CompilerParams(
-            collective_id=3, has_side_effects=True, vmem_limit_bytes=40 * 2**20
-        ),
-        name="reduce_weight",
-    )(part)
+    bufs = [
+        pltpu.VMEM((half, width), BF),
+        pltpu.VMEM((half, width), BF),
+        pltpu.VMEM((groups, blk, width), BF),
+        pltpu.VMEM((blk, width), BF),
+        pltpu.VMEM((deep, blk, lanes), BF),
+        pltpu.VMEM((blk, lanes), BF),
+        pltpu.VMEM((blk, width), BF),
+        pltpu.VMEM((conv_half, width), F32),
+        pltpu.VMEM((conv_half, width), F32),
+        pltpu.VMEM((groups, 8, conv_lanes), F32),
+        pltpu.VMEM((deep, 8, conv_lanes), F32),
+        pltpu.VMEM((8, conv_lanes), F32),
+    ]
+    sems = [dma((2,))] * 2 + [dma((2, groups))] * 2 + [dma((2, deep))] * 2 + [dma((deep,))] * 2
+    sems += [dma((2, groups))] * 2 + [dma((2,))] * 2
+    return bufs, sems
 
 
 def local(query_proj, key_proj, value_proj, cotangent, out_weight, conv_weight, rec_starts):
@@ -907,9 +921,11 @@
     layer, back, weight_part, conv_part = convolve(
         rec_starts, mixed, out_weight, cotangent[0], conv_weight
     )
-    conv_grad = lax.psum(conv_part[:KERN], ("dp", "seq")) * factor
-    weight_grad = reduce_weight(weight_part, factor)
-    dq, dk, dv = backward(p, kf, qf, kt, aux, back, rows, width)
+    dq, dk, dv, weight_sum, conv_sum = backward(
+        p, kf, qf, kt, aux, back, weight_part, conv_part, rows
+    )
+    weight_grad = weight_sum.astype(F32) * factor
+    conv_grad = conv_sum[:KERN] * factor
     return layer[None], dq[None], dk[None], dv[None], weight_grad, conv_grad
 
 

time: 366 us -> 181 us (0.49)
  waiting for transfers between devices: 143 us -> 0 us
  Pallas kernels: 197 us -> 172 us
  between operations: 14.1 us -> 0.69 us
  local copies, waits for them, and re-layouts: 9.73 us -> 3 us
    psum x1 -> x0, waiting for transfers between devices: 143 us -> none  [local(): conv_grad = lax.psum(conv_part[:KERN], ('dp', 'seq')) * factor]
    pallas_call x2 -> x1, Pallas kernels: 107 us -> 81.6 us  [backward(): pl.pallas_call(body, out_shape=[shape((rows, width), BF)] * 3 + [shape((w...]
    unnamed x17 -> x14, local copies, waits for them, and re-layouts: 9.73 us -> 3 us
  transfers between devices with their start and end apart: 1 -> 0, of which waited for: 1 -> 0; matrix products, arithmetic and copies ran while one was open for 0% -> 0% of each run, Pallas kernels for 29% -> 0%
where the time goes in v2:
time: 181 us
  Pallas kernels  172 us (95%)
  other arithmetic  4.95 us (3%)
  local copies, waits for them, and re-layouts  3 us (2%)
    pallas_call x1, Pallas kernels, backward(): pl.pallas_call(body, out_shape=[shape((rows, width), BF)] * 3 + [shape((w...  81.6 us
    pallas_call x1, Pallas kernels, forward(): pl.pallas_call(fwd_kernel, out_shape=[shape((total // BLK, total, BLK), B...  59.9 us
    pallas_call x1, Pallas kernels, convolve(): pl.pallas_call(conv_kernel, out_shape=[shape((rows, width), BF), shape((n...  30.8 us
    mul x1, other arithmetic, local(): weight_grad = weight_sum.astype(F32) * factor  4.28 us

profile of v2, /device:TPU:1, one launch (start us, length us, event | category | flops | bytes accessed | tf_op | source)
XLA Modules:
  0.0 180.9 jit_solution(17542187990533878176)
XLA Ops:
  0.6 59.9 %attend.1 = (bf16[12,3072,256]{2,1,0:T(8,128)(2,1)}, bf16[3072,256]{1,0:T(8,128)(2,1)}, bf16[3072,256]{1,0:T(8,128)(2,1)}, bf16[64,3072]{1,0:T(8,128)(2,1)}, f32...) custom-call(s32[1,2]{1,0:T(1,128)} %starts.3, bf16[192,1024]{1,0:T(8,128)(2,1)} %bitcast.13, bf16[192,1024]{1,0:T(8,128)(2,1)} %bitcast.14, ...), custom_call_target="tpu_custom_call" | custom-call | tf_op jit(solution)/shard_map/attend/pallas_call | solution.py:268
  60.5 30.8 %convolve.1 = (bf16[192,1024]{1,0:T(8,128)(2,1)}, bf16[16,96,128]{2,1,0:T(8,128)(2,1)}, bf16[1024,1024]{1,0:T(8,128)(2,1)}, f32[32,1024]{1,0:T(8,128)}) custom-call(s32[1,2]{1,0:T(1,128)} %starts.3, bf16[192,1024]{1,0:T(8,128)(2,1)} %get-tuple-element.21.mixed_ref, bf16[1024,1024]{1,0:T(8,128)(2,1)} %w_ref.1, bf16[192,1024]{1,0:T(8,128)(2,1)} %bitcast.8, ...), custom_call_target="tpu_custom_call" | custom-call | tf_op jit(solution)/shard_map/convolve/pallas_call | solution.py:468
  91.4 81.6 %attend_back.1 = (bf16[192,1024]{1,0:T(8,128)(2,1)}, bf16[192,1024]{1,0:T(8,128)(2,1)}, bf16[192,1024]{1,0:T(8,128)(2,1)}, bf16[1024,1024]{1,0:T(8,128)(2,1)}, f32[32,1024]{1,0:T(8,128)}) custom-call(bf16[12,3072,256]{2,1,0:T(8,128)(2,1)} %get-tuple-element.23.p_hbm, bf16[3072,256]{1,0:T(8,128)(2,1)} %get-tuple-element.24.kf_ref, ...), custom_call_target="tpu_custom_call" | custom-call | tf_op jit(solution)/shard_map/attend_back/pallas_call | solution.py:697
  172.9 0.0 copy-start.4
  172.9 0.0 copy-start
  173.0 0.0 copy-start.3
  173.0 4.3 %convert_multiply_fusion = f32[1024,1024]{1,0:T(8,128)} fusion(bf16[1024,1024]{1,0:T(8,128)(2,1)} %get-tuple-element.34), kind=kLoop, calls=%fused_computation | loop fusion | flops 2097152 | bytes 6291456 | tf_op jit(solution)/shard_map/mul | solution.py:927
  177.3 0.0 copy-start.2
  177.3 0.0 copy-start.1
  177.3 0.0 copy-done.4
  177.3 0.7 slice_multiply_fusion
  177.9 0.0 copy-done
  177.9 0.7 copy.17
  178.7 0.0 copy-done.3
  178.7 0.7 copy.18
  179.4 0.0 copy-done.2
  179.4 0.7 copy.19
  180.2 0.0 copy-done.1
  180.2 0.7 copy.20
Async XLA Ops:
  172.9 4.3 %copy-start.4 = (f32[32,1024]{1,0:T(8,128)S(1)}, f32[32,1024]{1,0:T(8,128)}, u32[]{:S(2)}) copy-start(f32[32,1024]{1,0:T(8,128)} %get-tuple-element.35) | copy-start | bytes 393220
  172.9 5.0 %copy-start = (bf16[192,1024]{1,0:T(8,128)(2,1)S(1)}, bf16[192,1024]{1,0:T(8,128)(2,1)}, u32[]{:S(2)}) copy-start(bf16[192,1024]{1,0:T(8,128)(2,1)} %get-tuple-element.22) | copy-start | bytes 1179652
  173.0 5.7 %copy-start.3 = (bf16[192,1024]{1,0:T(8,128)(2,1)S(1)}, bf16[192,1024]{1,0:T(8,128)(2,1)}, u32[]{:S(2)}) copy-start(bf16[192,1024]{1,0:T(8,128)(2,1)} %get-tuple-element.31) | copy-start | bytes 1179652
  177.3 2.2 %copy-start.2 = (bf16[192,1024]{1,0:T(8,128)(2,1)S(1)}, bf16[192,1024]{1,0:T(8,128)(2,1)}, u32[]{:S(2)}) copy-start(bf16[192,1024]{1,0:T(8,128)(2,1)} %get-tuple-element.32) | copy-start | bytes 1179652
  177.3 2.9 %copy-start.1 = (bf16[192,1024]{1,0:T(8,128)(2,1)S(1)}, bf16[192,1024]{1,0:T(8,128)(2,1)}, u32[]{:S(2)}) copy-start(bf16[192,1024]{1,0:T(8,128)(2,1)} %get-tuple-element.33) | copy-start | bytes 1179652

commit v3 on v2

v3 whole, which is shorter than its diff:
```python
import functools

import jax
import jax.numpy as jnp
from jax import lax
from jax.experimental import pallas as pl
from jax.experimental.pallas import tpu as pltpu
from jax.sharding import PartitionSpec as P

HD = 64
KERN = 31
HALO = 32
BLK = 256
SUB = 3
BIG = 1e30
BF = jnp.bfloat16
F32 = jnp.float32
VM = pl.BlockSpec(memory_space=pltpu.VMEM)
SM = pl.BlockSpec(memory_space=pltpu.SMEM)
ANY = pl.BlockSpec(memory_space=pl.ANY)


def dot(a, b, ca=1, cb=0):
    return lax.dot_general(a, b, (((ca,), (cb,)), ((), ())), preferred_element_type=F32)


def low_lanes(rows):
    return lax.broadcasted_iota(jnp.int32, (rows, 128), 1) < HD


def swap(x):
    return pltpu.roll(x, HD, 1)


def pack_halves(x):
    half = x.shape[0] // 2
    low = low_lanes(half)
    top, bottom = x[:half], x[half:]
    return jnp.where(low, top, swap(bottom)), jnp.where(low, swap(top), bottom)


def unpack_halves(first, second):
    low = low_lanes(first.shape[0])
    return jnp.where(low, first, swap(second)), jnp.where(low, swap(first), second)


def greet(axes):
    barrier = pltpu.get_barrier_semaphore()
    total = 0
    for axis in axes:
        count = lax.axis_size(axis)
        me = lax.axis_index(axis)

        def signal(d, _, axis=axis, count=count, me=me):
            pl.semaphore_signal(barrier, inc=1, device_id={axis: lax.rem(me + d, count)})
            return 0

        lax.fori_loop(1, count, signal, 0)
        total += count - 1
    pl.semaphore_wait(barrier, total)


def rows_at(index, size):
    return pl.ds(pl.multiple_of(index * size, size), size)


def attend(
    starts, q_ref, k_ref, v_ref, mixed_out,
    qk_send, v_send, qk_recv, v_recv, kx, qx, vx, kt, vt, s_buf, p_buf, aux, mix_send, mix_recv,
    k_ss, k_rs, v_ss, v_rs, m_ss, m_rs,
):
    n = lax.axis_size("seq")
    me = lax.axis_index("seq")
    rows, width = q_ref.shape
    half = rows // 2
    total = n * rows
    chunks = total // BLK
    group = SUB * BLK
    groups = total // group
    early = groups // 2
    owners = group // rows
    for t in range(width // 128):
        cols = pl.ds(t * 128, 128)
        q_, k_ = q_ref[:, cols].astype(F32) * (HD**-0.5), k_ref[:, cols].astype(F32)
        low = low_lanes(rows)
        qk_send[2 * t] = jnp.where(low, q_, swap(k_)).astype(BF)
        qk_send[2 * t + 1] = jnp.where(low, swap(q_), k_).astype(BF)
        first, second = pack_halves(v_ref[:, cols].astype(F32))
        v_send[2 * t] = first.astype(BF)
        v_send[2 * t + 1] = second.astype(BF)
    greet(("seq", "dp"))

    def qk_copy(peer, owner, dst_dev):
        return pltpu.make_async_remote_copy(
            src_ref=qk_send.at[peer],
            dst_ref=qk_recv.at[owner],
            send_sem=k_ss.at[peer],
            recv_sem=k_rs.at[owner],
            device_id={"seq": dst_dev},
        )

    def v_copy(peer, owner, dst_dev):
        return pltpu.make_async_remote_copy(
            src_ref=v_send.at[peer],
            dst_ref=v_recv.at[owner],
            send_sem=v_ss.at[peer],
            recv_sem=v_rs.at[owner],
            device_id={"seq": dst_dev},
        )

    def start_qk(d, _):
        peer = lax.rem(me + d, n)
        qk_copy(peer, me, peer).start()
        return 0

    def start_v(d, _):
        peer = lax.rem(me + d, n)
        v_copy(peer, me, peer).start()
        return 0

    lax.fori_loop(1, n, start_qk, 0)
    lax.fori_loop(1, n, start_v, 0)
    second = starts[0, 1]

    def take_qk(src):
        at = lax.broadcasted_iota(jnp.int32, (rows, 128), 0) + src * rows
        lane = lax.broadcasted_iota(jnp.int32, (rows, 128), 1) - HD
        later = jnp.where(at >= second, 1.0, 0.0)
        own = jnp.where(lane == 0, 1.0 - later, jnp.where(lane == 1, later, 0.0))
        other = jnp.where(lane == 0, later, jnp.where(lane == 1, 1.0 - later, 0.0)) * (-BIG)
        x = qk_recv[src].astype(F32)
        qx[rows_at(src, rows), :] = jnp.where(lane < 0, x, own).astype(BF)
        kx[rows_at(src, rows), :] = jnp.where(lane < 0, swap(x), other).astype(BF)

    qk_recv[me] = qk_send[me]
    take_qk(me)

    def arrive(d, _):
        src = lax.rem(me - d + n, n)
        qk_copy(me, src, me).wait_recv()
        take_qk(src)
        return 0

    lax.fori_loop(1, n, arrive, 0)
    def scores(c, q_blk):
        return dot(kx[c * BLK : (c + 1) * BLK, :], q_blk, 1, 1)

    def col_max(best, s):
        return jnp.maximum(best, jnp.max(s.reshape(BLK // 8, 8, BLK), axis=0))

    first_group = me // (n // groups)
    low_start = jnp.full((8, BLK), -3e38, F32)
    q_blk = qx[rows_at(first_group * SUB, BLK), :]
    best = low_start
    for c in range(chunks):
        s = scores(c, q_blk)
        s_buf[0, c * BLK : (c + 1) * BLK, :] = s
        best = col_max(best, s)

    def mix_copy(peer, owner, dst_dev):
        return pltpu.make_async_remote_copy(
            src_ref=mix_send.at[peer],
            dst_ref=mix_recv.at[owner],
            send_sem=m_ss.at[peer],
            recv_sem=m_rs.at[owner],
            device_id={"seq": dst_dev},
        )

    def finish_block(at, acc):
        inverse = 1.0 / acc[HD : HD + 1]
        mixed = (acc[:HD] * inverse).astype(BF).astype(F32)
        both = jnp.concatenate([jnp.broadcast_to(inverse, (HD, BLK)), mixed], axis=0)
        aux[rows_at(at, BLK), :] = both.T

    def send_group(g):
        for w in range(owners):
            owner = g * owners + w
            top = aux[rows_at(2 * owner, half), :]
            bottom = aux[rows_at(2 * owner + 1, half), :]
            packed = jnp.where(low_lanes(half), swap(top), bottom).astype(BF)
            mix_send[owner] = packed

            @pl.when(owner != me)
            def _():
                mix_copy(owner, me, owner).start()

            @pl.when(owner == me)
            def _():
                mix_recv[owner] = mix_send[owner]

    def one_group(i, m, with_values):
        g = lax.rem(first_group + i, groups)
        g_next = lax.rem(first_group + i + 1, groups)
        for sub in range(SUB):
            at = g * SUB + sub
            ahead = (sub + 1) % SUB
            next_at = at + 1 if sub + 1 < SUB else g_next * SUB
            q_next = qx[rows_at(next_at, BLK), :]
            best = low_start
            acc = jnp.zeros((HD + 16, BLK), F32)
            for c in range(chunks):
                cut = slice(c * BLK, (c + 1) * BLK)
                s = scores(c, q_next)
                s_buf[ahead, cut, :] = s
                best = col_max(best, s)
                p = jnp.exp(s_buf[sub, cut, :] - m).astype(BF)
                p_buf[at, cut, :] = p
                if with_values:
                    acc = acc + dot(vt[:, cut], p)
            m = jnp.max(best, axis=0, keepdims=True)
            if with_values:
                finish_block(at, acc)
        if with_values:
            send_group(g)
        return m

    m = lax.fori_loop(
        0, early, functools.partial(one_group, with_values=False), jnp.max(best, axis=0, keepdims=True)
    )
    v_recv[me] = v_send[me]

    def take_v(src):
        lane = lax.broadcasted_iota(jnp.int32, (half, 128), 1) - HD
        ones = jnp.where((lane >= 0) & (lane < 3), 1.0, 0.0)
        x = v_recv[src].astype(F32)
        vx[rows_at(2 * src, half), :] = jnp.where(lane < 0, x, ones).astype(BF)
        vx[rows_at(2 * src + 1, half), :] = jnp.where(lane < 0, swap(x), ones).astype(BF)

    take_v(me)

    def arrive_v(d, _):
        src = lax.rem(me - d + n, n)
        v_copy(me, src, me).wait_recv()
        take_v(src)
        return 0

    lax.fori_loop(1, n, arrive_v, 0)
    vt[HD : HD + 16, :] = jnp.ones((16, total), BF)
    for c in range(chunks):
        cut = slice(c * BLK, (c + 1) * BLK)
        vt[0:HD, cut] = vx[cut, :].T[:HD]

    def late_values(i, _):
        g = lax.rem(first_group + i, groups)
        for sub in range(SUB):
            acc = jnp.zeros((HD + 16, BLK), F32)
            for c in range(chunks):
                cut = slice(c * BLK, (c + 1) * BLK)
                acc = acc + dot(vt[:, cut], p_buf[g * SUB + sub, cut, :])
            finish_block(g * SUB + sub, acc)
        send_group(g)
        return 0

    lax.fori_loop(0, early, late_values, 0)
    lax.fori_loop(early, groups, functools.partial(one_group, with_values=True), m)
    for c in range(chunks):
        cut = slice(c * BLK, (c + 1) * BLK)
        kt[:, cut] = kx[cut, :].T[:HD]
    def settle(d, _):
        peer = lax.rem(me + d, n)
        qk_copy(peer, me, peer).wait_send()
        v_copy(peer, me, peer).wait_send()
        mix_copy(peer, me, peer).wait_send()
        mix_copy(me, lax.rem(me - d + n, n), me).wait_recv()
        return 0

    lax.fori_loop(1, n, settle, 0)
    for t in range(width // 128):
        top, bottom = unpack_halves(mix_recv[2 * t].astype(F32), mix_recv[2 * t + 1].astype(F32))
        mixed_out[0:half, t * 128 : (t + 1) * 128] = top.astype(BF)
        mixed_out[half:rows, t * 128 : (t + 1) * 128] = bottom.astype(BF)


def convolve(
    starts, mixed_ref, w_ref, cot_ref, taps_ref, layer_out, sums_out, csums_out, start_reduction,
    wpart, cpart, one, conv_one, proj, halo_recv, pad, head, ahead_recv, cpad, pb, back_send, back_recv,
    h_ss, h_rs, a_ss, a_rs, b_ss, b_rs, c_ss, c_rs,
):
    n = lax.axis_size("seq")
    me = lax.axis_index("seq")
    rows, width = mixed_ref.shape
    groups = rows // 8
    edge = HALO // 8
    total = n * rows
    second = starts[0, 1]
    base = me * rows
    right, left = lax.rem(me + 1, n), lax.rem(me + n - 1, n)
    step = 256
    for t in range(width // step):
        cut = pl.ds(t * step, step)
        out = dot(mixed_ref[...], w_ref[:, cut]).astype(BF)
        proj[:, cut] = out
        pad[0, HALO : HALO + rows, cut] = out.astype(F32)
    halo = pltpu.make_async_remote_copy(
        src_ref=proj.at[pl.ds(rows - HALO, HALO)],
        dst_ref=halo_recv,
        send_sem=h_ss,
        recv_sem=h_rs,
        device_id={"seq": right},
    )
    halo.start()

    def frame(first, count):
        return lax.broadcasted_iota(jnp.int32, (count, width), 0) + first

    pad[1, HALO : HALO + rows, :] = jnp.where(
        frame(base, rows) >= second, pad[0, HALO : HALO + rows, :], 0.0
    )

    def later(g):
        return (base + 8 * g >= second).astype(jnp.int32)

    def conv_groups(which):
        def one_tile(t, _):
            cut = rows_at(t, 128)
            w = [jnp.broadcast_to(taps_ref[j : j + 1, cut], (8, 128)) for j in range(KERN)]
            for g in which:
                acc = jnp.zeros((8, 128), F32)
                lab = later(g)
                for j in range(KERN):
                    acc = acc + w[j] * pad[lab, 8 * g + j + 2 : 8 * g + j + 10, cut]
                gate = jax.nn.sigmoid(acc)
                here = slice(8 * g, 8 * g + 8)
                layer = pad[0, HALO + 8 * g : HALO + 8 * g + 8, cut] + acc * gate
                head[here, cut] = layer
                cot = cot_ref[here, cut].astype(F32)
                back = cot * (gate * (1.0 + acc * (1.0 - gate)))
                cpad[1, here, cut] = back
                cpad[0, here, cut] = jnp.where(base + 8 * g < second, back, 0.0)
            return 0

        lax.fori_loop(0, width // 128, one_tile, 0)

    conv_groups(range(edge, groups))
    halo.wait_recv()
    before = halo_recv[...].astype(F32)
    pad[0, 0:HALO, :] = jnp.where(me > 0, before, 0.0)
    pad[1, 0:HALO, :] = jnp.where(
        (frame(base - HALO, HALO) >= second) & (me > 0), before, 0.0
    )
    conv_groups(range(edge))
    pb[0:HALO, :] = cpad[1, 0:HALO, :].astype(BF)
    ahead = pltpu.make_async_remote_copy(
        src_ref=pb.at[pl.ds(0, HALO)],
        dst_ref=ahead_recv,
        send_sem=a_ss,
        recv_sem=a_rs,
        device_id={"seq": left},
    )
    ahead.start()
    layer_out[...] = head[...].astype(BF)

    def spread_groups(which):
        def one_tile(t, _):
            cut = rows_at(t, 128)
            w = [jnp.broadcast_to(taps_ref[j : j + 1, cut], (8, 128)) for j in range(KERN)]
            for g in which:
                acc = cot_ref[8 * g : 8 * g + 8, cut].astype(F32)
                lab = later(g)
                for j in range(KERN):
                    acc = acc + w[j] * cpad[lab, 8 * g + 30 - j : 8 * g + 38 - j, cut]
                head[8 * g : 8 * g + 8, cut] = acc
            return 0

        lax.fori_loop(0, width // 128, one_tile, 0)

    spread_groups(range(groups - edge))
    ahead.wait()
    after = ahead_recv[...].astype(F32)
    inside = me < n - 1
    cpad[1, rows : rows + HALO, :] = jnp.where(inside, after, 0.0)
    cpad[0, rows : rows + HALO, :] = jnp.where(
        (frame(base + rows, HALO) < second) & inside, after, 0.0
    )
    spread_groups(range(groups - edge, groups))
    pb[...] = head[...].astype(BF)
    for t in range(width // step):
        out = dot(pb[...], w_ref[t * step : (t + 1) * step, :], 1, 1).astype(BF).astype(F32)
        for u in range(step // 128):
            first, second_ = pack_halves(out[:, u * 128 : (u + 1) * 128])
            at = 2 * (t * (step // 128) + u)
            back_send[at] = first.astype(BF)
            back_send[at + 1] = second_.astype(BF)

    def back_copy(peer, owner, dst_dev):
        return pltpu.make_async_remote_copy(
            src_ref=back_send.at[peer],
            dst_ref=back_recv.at[owner],
            send_sem=b_ss.at[peer],
            recv_sem=b_rs.at[owner],
            device_id={"seq": dst_dev},
        )

    def start(d, _):
        peer = lax.rem(me + d, n)
        back_copy(peer, me, peer).start()
        return 0

    lax.fori_loop(1, n, start, 0)
    back_recv[me] = back_send[me]
    for t in range(width // step):
        cut = pl.ds(t * step, step)
        wpart[cut, :] = dot(mixed_ref[:, cut], pb[...], 0, 0).astype(BF)
    core = lax.rem(me, 2)
    sibling = me + 1 - 2 * core
    part, conv_part = width // 2, (KERN + 1) // 2
    pair = pltpu.make_async_remote_copy(
        src_ref=wpart.at[rows_at(1 - core, part), :],
        dst_ref=one,
        send_sem=c_ss.at[0],
        recv_sem=c_rs.at[0],
        device_id={"seq": sibling},
    )
    pair.start()

    def tap_tile(t, _):
        cut = rows_at(t, 128)
        acc = [jnp.zeros((8, 128), F32)] * KERN
        for g in range(groups):
            lab = later(g)
            signal = cpad[1, 8 * g : 8 * g + 8, cut]
            for j in range(KERN):
                acc[j] = acc[j] + signal * pad[lab, 8 * g + j + 2 : 8 * g + j + 10, cut]
        for j in range(KERN):
            cpart[j : j + 1, cut] = jnp.sum(acc[j], axis=0, keepdims=True)
        cpart[KERN:, cut] = jnp.zeros((1, 128), F32)
        return 0

    lax.fori_loop(0, width // 128, tap_tile, 0)
    conv_pair = pltpu.make_async_remote_copy(
        src_ref=cpart.at[rows_at(1 - core, conv_part), :],
        dst_ref=conv_one,
        send_sem=c_ss.at[1],
        recv_sem=c_rs.at[1],
        device_id={"seq": sibling},
    )
    conv_pair.start()
    pair.wait()

    def add(i, _):
        own = wpart[pl.ds(pl.multiple_of(core * part + i * 32, 32), 32), :].astype(F32)
        sums_out[rows_at(i, 32), :] = (own + one[rows_at(i, 32), :].astype(F32)).astype(BF)
        return 0

    lax.fori_loop(0, part // 32, add, 0)
    conv_pair.wait()
    csums_out[...] = cpart[rows_at(core, conv_part), :] + conv_one[...]
    start_reduction()
    halo.wait_send()

    def settle(d, _):
        peer = lax.rem(me + d, n)
        back_copy(peer, me, peer).wait_send()
        back_copy(me, lax.rem(me - d + n, n), me).wait_recv()
        return 0

    lax.fori_loop(1, n, settle, 0)


def attend_back(
    p_buf, vx, qx, kt, aux, back, kv_recv, q_recv, steps,
    of, qd, s_buf, dqt, kv_send, q_send, kv_ss, kv_rs, q_ss, q_rs,
):
    n = lax.axis_size("seq")
    me = lax.axis_index("seq")
    rows = kv_recv.shape[1]
    half = rows // 2
    total = n * rows
    chunks = total // BLK
    group = SUB * BLK
    groups = total // group
    owners = group // rows
    first_group = me // (n // groups)
    first_chunk = first_group * SUB

    def prepare(p, _):
        x = back[p].astype(F32)
        low = low_lanes(half)
        lane = lax.broadcasted_iota(jnp.int32, (half, 128), 1) - HD
        for side in range(2):
            at = rows_at(2 * p + side, half)
            side_aux = aux[at, :]
            got = jnp.where(low, (x if side == 0 else swap(x)) * side_aux, 0.0)
            got = got.astype(BF).astype(F32)
            delta = -jnp.sum(got * swap(side_aux), axis=1, keepdims=True)
            top = delta.astype(BF).astype(F32)
            mid = (delta - top).astype(BF).astype(F32)
            rest = delta - top - mid
            feat = jnp.where(
                lane == 0, top, jnp.where(lane == 1, mid, jnp.where(lane == 2, rest, 0.0))
            )
            of[at, :] = jnp.where(low, got, feat).astype(BF)
            qd[at, :] = jnp.where(low, qx[at, :].astype(F32), swap(got)).astype(BF)
        return 0

    lax.fori_loop(0, n, prepare, 0)
    dqt[...] = jnp.zeros_like(dqt)
    places = {2: 1, 3: 2, 4: 3} if groups >= 4 else {0: 1, 1: 2, 2: 3}
    acc_k, acc_v = s_buf.at[1, 0:group, 0:128], s_buf.at[1, 0:group, 128:256]
    halves = chunks % 4 == 0

    def kv_copy(peer, owner, dst_dev):
        return pltpu.make_async_remote_copy(
            src_ref=kv_send.at[peer],
            dst_ref=kv_recv.at[owner],
            send_sem=kv_ss.at[peer],
            recv_sem=kv_rs.at[owner],
            device_id={"seq": dst_dev},
        )

    def q_copy(peer, owner, dst_dev):
        return pltpu.make_async_remote_copy(
            src_ref=q_send.at[peer],
            dst_ref=q_recv.at[owner],
            send_sem=q_ss.at[peer],
            recv_sem=q_rs.at[owner],
            device_id={"seq": dst_dev},
        )

    def send_q(side):
        def turn(j, _):
            c = lax.rem(first_chunk + j, chunks)
            x = dqt[:, rows_at(c, BLK)] * (HD**-0.5)
            aux[rows_at(c, BLK), :] = jnp.concatenate([x, jnp.zeros_like(x)], axis=0).T
            return 0

        lax.fori_loop(side * chunks // 2, (side + 1) * chunks // 2, turn, 0)

        def send(d, _):
            owner = lax.rem(first_group * owners + d, n)
            top = aux[rows_at(2 * owner, half), :]
            bottom = aux[rows_at(2 * owner + 1, half), :]
            q_send[owner] = jnp.where(low_lanes(half), top, swap(bottom)).astype(BF)

            @pl.when(owner != me)
            def _():
                q_copy(owner, me, owner).start()

            @pl.when(owner == me)
            def _():
                q_recv[owner] = q_send[owner]

            return 0

        lax.fori_loop(side * n // 2, (side + 1) * n // 2, send, 0)

    def one_group(i, _):
        g = lax.rem(first_group + i, groups)
        acc_k[...] = jnp.zeros_like(acc_k)
        acc_v[...] = jnp.zeros_like(acc_v)

        def prob_back(r, c):
            return dot(vx[rows_at(g * SUB + r, BLK), :], of[rows_at(c, BLK), :], 1, 1)

        for r in range(SUB):
            s_buf[0, r * BLK : (r + 1) * BLK, :] = prob_back(r, first_chunk)

        def two_chunks(pair, _):
            for par in range(2):
                c = lax.rem(2 * pair + par + first_chunk, chunks)
                ahead = lax.rem(c + 1, chunks)
                q_d = qd[rows_at(c, BLK), :]
                dq = jnp.zeros((HD, BLK), F32)
                for r in range(SUB):
                    cut = slice(r * BLK, (r + 1) * BLK)
                    keys = rows_at(g * SUB + r, BLK)
                    there = slice((1 - par) * group + r * BLK, (1 - par) * group + (r + 1) * BLK)
                    here = slice(par * group + r * BLK, par * group + (r + 1) * BLK)
                    s_buf[0, there, :] = prob_back(r, ahead)
                    p = p_buf[c, keys, :]
                    ds = (p.astype(F32) * s_buf[0, here, :]).astype(BF)
                    acc_v[cut, :] += dot(p, q_d)
                    acc_k[cut, :] += dot(ds, q_d)
                    dq = dq + dot(kt[:, keys], ds)
                dqt[:, rows_at(c, BLK)] += dq
            return 0

        for h in range(2):
            lax.fori_loop(h * chunks // 4, (h + 1) * chunks // 4, two_chunks, 0)
            for place, number in places.items():
                if place % 2 == h:
                    pl.when(i == place // 2)(steps[number])
            if h == 0 and halves:
                pl.when(i == groups - 1)(functools.partial(send_q, 0))
        for w in range(owners):
            owner = g * owners + w
            cut = slice(w * rows, (w + 1) * rows)
            kv_send[owner] = jnp.where(low_lanes(rows), acc_k[cut, :], acc_v[cut, :]).astype(BF)

            @pl.when(owner != me)
            def _():
                kv_copy(owner, me, owner).start()

            @pl.when(owner == me)
            def _():
                kv_recv[owner] = kv_send[owner]

        return 0

    lax.fori_loop(0, groups, one_group, 0)
    for side in range(1 if halves else 0, 2):
        send_q(side)

    def settle_kv(d, _):
        peer = lax.rem(me + d, n)
        kv_copy(peer, me, peer).wait_send()
        kv_copy(me, lax.rem(me - d + n, n), me).wait_recv()
        return 0

    lax.fori_loop(1, n, settle_kv, 0)
    steps[4]()

    def settle_q(d, _):
        peer = lax.rem(me + d, n)
        q_copy(peer, me, peer).wait_send()
        q_copy(me, lax.rem(me - d + n, n), me).wait_recv()
        return 0

    lax.fori_loop(1, n, settle_q, 0)
    steps[5]()


def layer_kernel(
    starts, q_ref, k_ref, v_ref, w_hbm, cot_hbm, taps_hbm,
    layer_out, kv_recv, q_recv, w_out, conv_out,
    w_ref, cot_ref, taps_ref, mixed, sums, conv_sums,
    kx, qx, vx, kt, s_buf, p_buf, aux, back_recv, in_sem, *rest,
):
    rest = list(rest)

    def take(count):
        taken = rest[:count]
        del rest[:count]
        return taken

    loads = [
        pltpu.make_async_copy(w_hbm, w_ref, in_sem.at[0]),
        pltpu.make_async_copy(cot_hbm, cot_ref, in_sem.at[1]),
        pltpu.make_async_copy(taps_hbm, taps_ref, in_sem.at[2]),
    ]
    for load in loads:
        load.start()
    qk_send, v_send, qk_recv, v_recv, vt, mix_send, mix_recv = take(7)
    attend(
        starts, q_ref, k_ref, v_ref, mixed,
        qk_send, v_send, qk_recv, v_recv, kx, qx, vx, kt, vt, s_buf, p_buf, aux, mix_send, mix_recv,
        *take(6),
    )
    for load in loads:
        load.wait()
    bufs = take(12)
    sems = take(8)
    reduce_bufs = take(8)
    steps = reducer(sums, conv_sums, w_out, conv_out, reduce_bufs, take(10))
    convolve(
        starts, mixed, w_ref, cot_ref, taps_ref, layer_out, sums, conv_sums, steps[0],
        *bufs, back_recv, *sems,
    )
    of, qd, dqt, kv_send, q_send = take(5)
    attend_back(
        p_buf, vx, qx, kt, aux, back_recv, kv_recv, q_recv, steps,
        of, qd, s_buf, dqt, kv_send, q_send, *rest,
    )


def layer(starts, q, k, v, weight, cot, taps):
    rows, width = q.shape
    n, groups = lax.axis_size("seq"), lax.axis_size("dp")
    total, half = n * rows, rows // 2
    shape, vmem, dma = jax.ShapeDtypeStruct, pltpu.VMEM, pltpu.SemaphoreType.DMA
    bufs, sems = reducer_bufs(width, n, groups)
    wide, narrow = vmem((n, rows, 128), BF), vmem((n, half, 128), BF)
    per_peer = dma((n,))
    return pl.pallas_call(
        layer_kernel,
        out_shape=[
            shape((rows, width), BF),
            shape((n, rows, 128), BF),
            shape((n, half, 128), BF),
            shape((width, width), BF),
            shape((KERN + 1, width), F32),
        ],
        in_specs=[SM, VM, VM, VM, ANY, ANY, ANY],
        out_specs=[VM] * 5,
        scratch_shapes=[
            vmem((width, width), BF), vmem((rows, width), BF), vmem((KERN, width), F32),
            vmem((rows, width), BF),
            vmem((width // 2, width), BF), vmem(((KERN + 1) // 2, width), F32),
            vmem((total, 128), BF), vmem((total, 128), BF), vmem((total, 128), BF),
            vmem((HD, total), BF),
            vmem((SUB, total, BLK), F32), vmem((total // BLK, total, BLK), BF),
            vmem((total, 128), F32), narrow, dma((3,)),
            wide, narrow, wide, narrow, vmem((HD + 16, total), BF), narrow, narrow,
            *[per_peer] * 6,
            vmem((width, width), BF), vmem((KERN + 1, width), F32),
            vmem((width // 2, width), BF), vmem(((KERN + 1) // 2, width), F32),
            vmem((rows, width), BF), vmem((HALO, width), BF), vmem((2, rows + HALO, width), F32),
            vmem((rows, width), F32), vmem((HALO, width), BF), vmem((2, rows + HALO, width), F32),
            vmem((rows, width), BF), narrow,
            dma, dma, dma, dma, per_peer, per_peer, dma((2,)), dma((2,)),
            *bufs, *sems,
            vmem((total, 128), BF), vmem((total, 128), BF), vmem((HD, total), F32), wide, narrow,
            *[per_peer] * 4,
        ],
        compiler_params=pltpu.CompilerParams(
            collective_id=0, has_side_effects=True, vmem_limit_bytes=62 * 2**20 - 2**19
        ),
        name="layer",
    )(starts, q, k, v, weight, cot, taps)


def finish_kernel(
    factor, kv_ref, q_ref, layer_ref, w_ref, conv_ref, layer_out, dq_out, dk_out, dv_out, w_out, conv_out
):
    rows = kv_ref.shape[1]
    half = rows // 2
    low = low_lanes(rows)
    one, two = kv_ref[0].astype(F32), kv_ref[1].astype(F32)
    dk_out[...] = jnp.where(low, one, swap(two)).astype(BF)
    dv_out[...] = jnp.where(low, swap(one), two).astype(BF)
    top, bottom = unpack_halves(q_ref[0].astype(F32), q_ref[1].astype(F32))
    dq_out[0:half, :] = top.astype(BF)
    dq_out[half:rows, :] = bottom.astype(BF)
    layer_out[...] = layer_ref[...]
    w_out[...] = w_ref[...].astype(F32) * factor
    conv_out[...] = conv_ref[0:KERN, :] * factor


def finish(kv, q, layer, w_sum, conv_sum, factor):
    rows, width = layer.shape
    steps = width // 128
    shape = jax.ShapeDtypeStruct
    column = pl.BlockSpec((rows, 128), lambda t: (0, t))
    band = pl.BlockSpec((width // steps, width), lambda t: (t, 0))
    return pl.pallas_call(
        functools.partial(finish_kernel, factor),
        grid=(steps,),
        out_shape=[shape((rows, width), BF)] * 4
        + [shape((width, width), F32), shape((KERN, width), F32)],
        in_specs=[
            pl.BlockSpec((2, rows, 128), lambda t: (t, 0, 0)),
            pl.BlockSpec((2, rows // 2, 128), lambda t: (t, 0, 0)),
            column,
            band,
            pl.BlockSpec((KERN + 1, 128), lambda t: (0, t)),
        ],
        out_specs=[column] * 4 + [band, pl.BlockSpec((KERN, 128), lambda t: (0, t))],
        name="finish",
    )(kv, q, layer, w_sum, conv_sum)


def reducer(sums, conv_sums, w_out, conv_out, bufs, sems):
    two, mine, three, part, four, conv_two, conv_three, conv_part = bufs
    s2, r2, s3, r3, s4, r4, s5, r5, s6, r6 = sems
    n, groups = lax.axis_size("seq"), lax.axis_size("dp")
    me, dp = lax.axis_index("seq"), lax.axis_index("dp")
    width = w_out.shape[0]
    core, z = lax.rem(me, 2), me // 2
    deep = n // 2
    half = width // 2
    blk = half // groups
    lanes = width // deep
    conv_half = (KERN + 1) // 2
    per_row = groups // 2
    conv_lanes = width // per_row
    sibling = me + 1 - 2 * core

    def send(src, dst, ss, rs, dev):
        return pltpu.make_async_remote_copy(
            src_ref=src, dst_ref=dst, send_sem=ss, recv_sem=rs, device_id=dev
        )

    def tile(ref, index, first=0):
        row = pl.multiple_of(first + 8 * (index // per_row), 8)
        return ref.at[pl.ds(row, 8), rows_at(lax.rem(index, per_row), conv_lanes)]

    def c2(peer, owner, dev):
        dev = {"dp": dev}
        return (
            send(sums.at[rows_at(peer, blk), :], two.at[owner], s2.at[0, peer], r2.at[0, owner], dev),
            send(tile(conv_sums, peer), conv_two.at[owner], s2.at[1, peer], r2.at[1, owner], dev),
        )

    def c3(peer, owner, dev):
        dev = {"seq": dev * 2 + core}
        return (
            send(mine.at[:, rows_at(peer, lanes)], three.at[owner], s3.at[0, peer], r3.at[0, owner], dev),
            send(conv_part, conv_three.at[owner], s3.at[1, peer], r3.at[1, owner], dev),
        )

    def c4(peer, owner, dev):
        dev = {"seq": dev * 2 + core}
        return (send(part, four.at[:, rows_at(owner, lanes)], s4.at[peer], r4.at[owner], dev),)

    def c5(peer, owner, dev):
        dev = {"dp": dev}
        to = w_out.at[rows_at(core * groups + owner, blk), :]
        return (
            send(four, to, s5.at[0, peer], r5.at[0, owner], dev),
            send(conv_part, tile(conv_out, owner, core * conv_half), s5.at[1, peer], r5.at[1, owner], dev),
        )

    def c6(owner):
        dev = {"seq": sibling}
        here, there = w_out.at[rows_at(owner, half), :], conv_out.at[rows_at(owner, conv_half), :]
        return send(here, here, s6.at[0], r6.at[0], dev), send(there, there, s6.at[1], r6.at[1], dev)

    def to_all(copies, own, count):
        def go(d, _):
            peer = lax.rem(own + d, count)
            for copy in copies(peer, own, peer):
                copy.start()
            return 0

        lax.fori_loop(1, count, go, 0)

    def from_all(copies, own, count):
        def go(d, _):
            for copy in copies(own, lax.rem(own - d + count, count), own):
                copy.wait_recv()
            return 0

        lax.fori_loop(1, count, go, 0)

    def step1():
        to_all(c2, dp, groups)

    def step2():
        from_all(c2, dp, groups)
        two[dp] = sums[rows_at(dp, blk), :]
        conv_two[dp] = tile(conv_sums, dp)[...]

        def add(i, total):
            return total[0] + two[i].astype(F32), total[1] + conv_two[i]

        zero = jnp.zeros((blk, width), F32), jnp.zeros((8, conv_lanes), F32)
        total = lax.fori_loop(0, groups, add, zero)
        mine[...] = total[0].astype(BF)
        conv_part[...] = total[1]
        to_all(c3, z, deep)

    def step3():
        from_all(c3, z, deep)
        three[z] = mine[:, rows_at(z, lanes)]
        conv_three[z] = conv_part[...]
        total, conv_total = jnp.zeros((blk, lanes), F32), jnp.zeros((8, conv_lanes), F32)
        for i in range(deep):
            total = total + three[i].astype(F32)
            conv_total = conv_total + conv_three[i]
        part[...] = total.astype(BF)
        four[:, rows_at(z, lanes)] = part[...]

        def settle(d, _):
            c3(lax.rem(z + d, deep), z, lax.rem(z + d, deep))[1].wait_send()
            return 0

        lax.fori_loop(1, deep, settle, 0)
        conv_part[...] = conv_total
        to_all(c4, z, deep)

    def step4():
        from_all(c4, z, deep)
        w_out[rows_at(core * groups + dp, blk), :] = four[...]
        tile(conv_out, dp, core * conv_half)[...] = conv_part[...]
        to_all(c5, dp, groups)

    def step5():
        from_all(c5, dp, groups)
        for copy in c6(core):
            copy.start()

    def step6():
        for copy in c6(1 - core):
            copy.wait_recv()
        for copy in c6(core):
            copy.wait_send()

        def settle_dp(d, _):
            peer = lax.rem(dp + d, groups)
            for copy in (*c2(peer, dp, peer), *c5(peer, dp, peer)):
                copy.wait_send()
            return 0

        lax.fori_loop(1, groups, settle_dp, 0)

        def settle_z(d, _):
            peer = lax.rem(z + d, deep)
            for copy in (c3(peer, z, peer)[0], *c4(peer, z, peer)):
                copy.wait_send()
            return 0

        lax.fori_loop(1, deep, settle_z, 0)

    return step1, step2, step3, step4, step5, step6


def reducer_bufs(width, n, groups):
    half, deep = width // 2, n // 2
    blk, lanes = half // groups, width // deep
    conv_lanes = width // (groups // 2)
    dma = pltpu.SemaphoreType.DMA
    bufs = [
        pltpu.VMEM((groups, blk, width), BF),
        pltpu.VMEM((blk, width), BF),
        pltpu.VMEM((deep, blk, lanes), BF),
        pltpu.VMEM((blk, lanes), BF),
        pltpu.VMEM((blk, width), BF),
        pltpu.VMEM((groups, 8, conv_lanes), F32),
        pltpu.VMEM((deep, 8, conv_lanes), F32),
        pltpu.VMEM((8, conv_lanes), F32),
    ]
    sems = [dma((2, groups))] * 2 + [dma((2, deep))] * 2 + [dma((deep,))] * 2
    sems += [dma((2, groups))] * 2 + [dma((2,))] * 2
    return bufs, sems


def local(query_proj, key_proj, value_proj, cotangent, out_weight, conv_weight, rec_starts):
    rows, width = query_proj.shape[1:]
    factor = (lax.axis_size("dp") * lax.axis_size("seq") * rows) ** -0.5
    out, kv, q, weight_sum, conv_sum = layer(
        rec_starts, query_proj[0], key_proj[0], value_proj[0], out_weight, cotangent[0], conv_weight
    )
    out, dq, dk, dv, weight_grad, conv_grad = finish(kv, q, out, weight_sum, conv_sum, factor)
    return out[None], dq[None], dk[None], dv[None], weight_grad, conv_grad


def solution(mesh):
    frames = P("dp", "seq", None)
    return jax.shard_map(
        local,
        mesh=mesh,
        in_specs=(frames, frames, frames, frames, P(), P(), P("dp", None)),
        out_specs=(frames, frames, frames, frames, P(), P()),
        check_vma=False,
    )
```

time: 181 us -> 147 us (0.81)
  Pallas kernels: 172 us -> 146 us
  other arithmetic: 4.95 us -> 0 us
  local copies, waits for them, and re-layouts: 3 us -> 0 us
    pallas_call x3 -> x2, Pallas kernels: 172 us -> 146 us  [the longest x1 139 us: layer(): pl.pallas_call(layer_kernel, out_shape=[shape((rows, width), BF), shape((...]
    mul x2 -> x0, other arithmetic: 4.95 us -> none  [the longest x1 4.28 us: local(): weight_grad = weight_sum.astype(F32) * factor]
    unnamed x14 -> x0, local copies, waits for them, and re-layouts: 3 us -> none
where the time goes in v3:
time: 147 us
  Pallas kernels  146 us (99%)
    pallas_call x1, Pallas kernels, layer(): pl.pallas_call(layer_kernel, out_shape=[shape((rows, width), BF), shape((...  139 us
    pallas_call x1, Pallas kernels, finish(): pl.pallas_call(functools.partial(finish_kernel, factor), grid=(steps,), o...  6.82 us

profile of v3, /device:TPU:1, one launch (start us, length us, event | category | flops | bytes accessed | tf_op | source)
XLA Modules:
  0.0 146.7 jit_solution(3155486414022351367)
XLA Ops:
  0.6 139.1 %layer.1 = (bf16[192,1024]{1,0:T(8,128)(2,1)}, bf16[16,192,128]{2,1,0:T(8,128)(2,1)}, bf16[16,96,128]{2,1,0:T(8,128)(2,1)}, bf16[1024,1024]{1,0:T(8,128)(2,1)}, f32[32,1024]{1,0:T(8,128)}) custom-call(s32[1,2]{1,0:T(1,128)} %starts.1, bf16[192,1024]{1,0:T(8,128)(2,1)} %bitcast.8, bf16[192,1024]{1,0:T(8,128)(2,1)} %bitcast.9, bf16[192,1024]{1,0:T(8,128)(2,1)} %bitcast.10, ...), custom_call_target="tpu_custom_call" | custom-call | tf_op jit(solution)/shard_map/layer/pallas_call | solution.py:674
  139.7 6.8 %finish.1 = (bf16[192,1024]{1,0:T(8,128)(2,1)}, bf16[192,1024]{1,0:T(8,128)(2,1)}, bf16[192,1024]{1,0:T(8,128)(2,1)}, bf16[192,1024]{1,0:T(8,128)(2,1)}, f32[1024,1024]{1,0:T(8,128)}, /*index=5*/f32[31,1024]{1,0:T(8,128)}) custom-call(bf16[16,192,128]{2,1,0:T(8,128)(2,1)} %get-tuple-element.17.kv_ref, bf16[16,96,128]{2,1,0:T(8,128)(2,1)} %get-tuple-element.18.q_ref, ...), custom_call_target="tpu_custom_call" | custom-call | tf_op jit(solution)/shard_map/finish/pallas_call | solution.py:735

commit v4 on v3

--- a/solution.py
+++ b/solution.py
@@ -12,6 +12,7 @@
 HALO = 32
 BLK = 256
 SUB = 3
+STEPS = 2
 BIG = 1e30
 BF = jnp.bfloat16
 F32 = jnp.float32
@@ -57,7 +58,27 @@
 
         lax.fori_loop(1, count, signal, 0)
         total += count - 1
-    pl.semaphore_wait(barrier, total)
+    return total
+
+
+def ring_order(n):
+    deep = n // 2
+    order = []
+    for far in range(deep // 2 - 1, 1, -1):
+        order += [(far, 0), (-far, 0), (far, 1), (-far, 1)]
+    order += [(deep // 2, 0), (0, 1), (deep // 2, 1), (0, 0)]
+    return order + [(1, 0), (-1, 0), (1, 1), (-1, 1)]
+
+
+def slot_owners(n):
+    me = lax.axis_index("seq")
+    core, z = lax.rem(me, 2), me // 2
+    deep = n // 2
+    owners = []
+    for steps, other in ring_order(n):
+        owner = 2 * lax.rem(z + (steps + deep) % deep, deep) + (1 - core if other else core)
+        owners.append((owner, steps == 0 and not other))
+    return owners
 
 
 def rows_at(index, size):
@@ -65,7 +86,7 @@
 
 
 def attend(
-    starts, q_ref, k_ref, v_ref, mixed_out,
+    starts, q_ref, k_ref, v_ref, loads, greeted, mixed_out,
     qk_send, v_send, qk_recv, v_recv, kx, qx, vx, kt, vt, s_buf, p_buf, aux, mix_send, mix_recv,
     k_ss, k_rs, v_ss, v_rs, m_ss, m_rs,
 ):
@@ -79,16 +100,16 @@
     groups = total // group
     early = groups // 2
     owners = group // rows
+    slots = slot_owners(n)
+    for load in loads[:2]:
+        load.wait()
     for t in range(width // 128):
         cols = pl.ds(t * 128, 128)
         q_, k_ = q_ref[:, cols].astype(F32) * (HD**-0.5), k_ref[:, cols].astype(F32)
         low = low_lanes(rows)
         qk_send[2 * t] = jnp.where(low, q_, swap(k_)).astype(BF)
         qk_send[2 * t + 1] = jnp.where(low, swap(q_), k_).astype(BF)
-        first, second = pack_halves(v_ref[:, cols].astype(F32))
-        v_send[2 * t] = first.astype(BF)
-        v_send[2 * t + 1] = second.astype(BF)
-    greet(("seq", "dp"))
+    pl.semaphore_wait(pltpu.get_barrier_semaphore(), greeted)
 
     def qk_copy(peer, owner, dst_dev):
         return pltpu.make_async_remote_copy(
@@ -108,49 +129,43 @@
             device_id={"seq": dst_dev},
         )
 
-    def start_qk(d, _):
-        peer = lax.rem(me + d, n)
-        qk_copy(peer, me, peer).start()
-        return 0
-
-    def start_v(d, _):
-        peer = lax.rem(me + d, n)
-        v_copy(peer, me, peer).start()
-        return 0
-
-    lax.fori_loop(1, n, start_qk, 0)
-    lax.fori_loop(1, n, start_v, 0)
+    for peer, own in slots:
+        if not own:
+            qk_copy(peer, me, peer).start()
+    loads[2].wait()
+    for t in range(width // 128):
+        first, second = pack_halves(v_ref[:, t * 128 : (t + 1) * 128].astype(F32))
+        v_send[2 * t] = first.astype(BF)
+        v_send[2 * t + 1] = second.astype(BF)
+    for peer, own in slots:
+        if not own:
+            v_copy(peer, me, peer).start()
     second = starts[0, 1]
 
-    def take_qk(src):
+    def take_qk(slot, src):
         at = lax.broadcasted_iota(jnp.int32, (rows, 128), 0) + src * rows
         lane = lax.broadcasted_iota(jnp.int32, (rows, 128), 1) - HD
         later = jnp.where(at >= second, 1.0, 0.0)
         own = jnp.where(lane == 0, 1.0 - later, jnp.where(lane == 1, later, 0.0))
         other = jnp.where(lane == 0, later, jnp.where(lane == 1, 1.0 - later, 0.0)) * (-BIG)
         x = qk_recv[src].astype(F32)
-        qx[rows_at(src, rows), :] = jnp.where(lane < 0, x, own).astype(BF)
-        kx[rows_at(src, rows), :] = jnp.where(lane < 0, swap(x), other).astype(BF)
+        qx[slot * rows : (slot + 1) * rows, :] = jnp.where(lane < 0, x, own).astype(BF)
+        kx[slot * rows : (slot + 1) * rows, :] = jnp.where(lane < 0, swap(x), other).astype(BF)
 
     qk_recv[me] = qk_send[me]
-    take_qk(me)
-
-    def arrive(d, _):
-        src = lax.rem(me - d + n, n)
-        qk_copy(me, src, me).wait_recv()
-        take_qk(src)
-        return 0
-
-    lax.fori_loop(1, n, arrive, 0)
+    for slot, (src, own) in enumerate(slots):
+        if not own:
+            qk_copy(me, src, me).wait_recv()
+        take_qk(slot, src)
+
     def scores(c, q_blk):
         return dot(kx[c * BLK : (c + 1) * BLK, :], q_blk, 1, 1)
 
     def col_max(best, s):
         return jnp.maximum(best, jnp.max(s.reshape(BLK // 8, 8, BLK), axis=0))
 
-    first_group = me // (n // groups)
     low_start = jnp.full((8, BLK), -3e38, F32)
-    q_blk = qx[rows_at(first_group * SUB, BLK), :]
+    q_blk = qx[0:BLK, :]
     best = low_start
     for c in range(chunks):
         s = scores(c, q_blk)
@@ -172,25 +187,24 @@
         both = jnp.concatenate([jnp.broadcast_to(inverse, (HD, BLK)), mixed], axis=0)
         aux[rows_at(at, BLK), :] = both.T
 
-    def send_group(g):
-        for w in range(owners):
-            owner = g * owners + w
-            top = aux[rows_at(2 * owner, half), :]
-            bottom = aux[rows_at(2 * owner + 1, half), :]
-            packed = jnp.where(low_lanes(half), swap(top), bottom).astype(BF)
-            mix_send[owner] = packed
-
-            @pl.when(owner != me)
-            def _():
+    def send_some(g):
+        for slot in range(g * owners, (g + 1) * owners):
+            owner, own = slots[slot]
+            top = aux[slot * rows : slot * rows + half, :]
+            bottom = aux[slot * rows + half : (slot + 1) * rows, :]
+            mix_send[owner] = jnp.where(low_lanes(half), swap(top), bottom).astype(BF)
+            if own:
+                mix_recv[owner] = mix_send[owner]
+            else:
                 mix_copy(owner, me, owner).start()
 
-            @pl.when(owner == me)
-            def _():
-                mix_recv[owner] = mix_send[owner]
+    def send_group(i):
+        for g in range(groups):
+            pl.when(i == g)(functools.partial(send_some, g))
 
     def one_group(i, m, with_values):
-        g = lax.rem(first_group + i, groups)
-        g_next = lax.rem(first_group + i + 1, groups)
+        g = i
+        g_next = lax.rem(i + 1, groups)
         for sub in range(SUB):
             at = g * SUB + sub
             ahead = (sub + 1) % SUB
@@ -218,30 +232,22 @@
         0, early, functools.partial(one_group, with_values=False), jnp.max(best, axis=0, keepdims=True)
     )
     v_recv[me] = v_send[me]
-
-    def take_v(src):
-        lane = lax.broadcasted_iota(jnp.int32, (half, 128), 1) - HD
-        ones = jnp.where((lane >= 0) & (lane < 3), 1.0, 0.0)
+    lane = lax.broadcasted_iota(jnp.int32, (half, 128), 1) - HD
+    ones = jnp.where((lane >= 0) & (lane < 3), 1.0, 0.0)
+    for slot, (src, own) in enumerate(slots):
+        if not own:
+            v_copy(me, src, me).wait_recv()
         x = v_recv[src].astype(F32)
-        vx[rows_at(2 * src, half), :] = jnp.where(lane < 0, x, ones).astype(BF)
-        vx[rows_at(2 * src + 1, half), :] = jnp.where(lane < 0, swap(x), ones).astype(BF)
-
-    take_v(me)
-
-    def arrive_v(d, _):
-        src = lax.rem(me - d + n, n)
-        v_copy(me, src, me).wait_recv()
-        take_v(src)
-        return 0
-
-    lax.fori_loop(1, n, arrive_v, 0)
+        at = slot * rows
+        vx[at : at + half, :] = jnp.where(lane < 0, x, ones).astype(BF)
+        vx[at + half : at + rows, :] = jnp.where(lane < 0, swap(x), ones).astype(BF)
     vt[HD : HD + 16, :] = jnp.ones((16, total), BF)
     for c in range(chunks):
         cut = slice(c * BLK, (c + 1) * BLK)
         vt[0:HD, cut] = vx[cut, :].T[:HD]
 
     def late_values(i, _):
-        g = lax.rem(first_group + i, groups)
+        g = i
         for sub in range(SUB):
             acc = jnp.zeros((HD + 16, BLK), F32)
             for c in range(chunks):
@@ -391,12 +397,9 @@
             device_id={"seq": dst_dev},
         )
 
-    def start(d, _):
-        peer = lax.rem(me + d, n)
-        back_copy(peer, me, peer).start()
-        return 0
-
-    lax.fori_loop(1, n, start, 0)
+    for peer, own in slot_owners(n):
+        if not own:
+            back_copy(peer, me, peer).start()
     back_recv[me] = back_send[me]
     for t in range(width // step):
         cut = pl.ds(t * step, step)
@@ -448,17 +451,19 @@
     start_reduction()
     halo.wait_send()
 
+    def arrived(src):
+        back_copy(me, src, me).wait_recv()
+
     def settle(d, _):
         peer = lax.rem(me + d, n)
         back_copy(peer, me, peer).wait_send()
-        back_copy(me, lax.rem(me - d + n, n), me).wait_recv()
         return 0
 
-    lax.fori_loop(1, n, settle, 0)
+    return arrived, lambda: lax.fori_loop(1, n, settle, 0)
 
 
 def attend_back(
-    p_buf, vx, qx, kt, aux, back, kv_recv, q_recv, steps,
+    p_buf, vx, qx, kt, aux, back, arrived, kv_recv, q_recv, copies, steps,
     of, qd, s_buf, dqt, kv_send, q_send, kv_ss, kv_rs, q_ss, q_rs,
 ):
     n = lax.axis_size("seq")
@@ -470,15 +475,14 @@
     group = SUB * BLK
     groups = total // group
     owners = group // rows
-    first_group = me // (n // groups)
-    first_chunk = first_group * SUB
-
-    def prepare(p, _):
-        x = back[p].astype(F32)
+    slots = slot_owners(n)
+
+    def prepare(slot, src):
+        x = back[src].astype(F32)
         low = low_lanes(half)
         lane = lax.broadcasted_iota(jnp.int32, (half, 128), 1) - HD
         for side in range(2):
-            at = rows_at(2 * p + side, half)
+            at = slice(slot * rows + side * half, slot * rows + (side + 1) * half)
             side_aux = aux[at, :]
             got = jnp.where(low, (x if side == 0 else swap(x)) * side_aux, 0.0)
             got = got.astype(BF).astype(F32)
@@ -491,11 +495,13 @@
             )
             of[at, :] = jnp.where(low, got, feat).astype(BF)
             qd[at, :] = jnp.where(low, qx[at, :].astype(F32), swap(got)).astype(BF)
-        return 0
-
-    lax.fori_loop(0, n, prepare, 0)
+
     dqt[...] = jnp.zeros_like(dqt)
-    places = {2: 1, 3: 2, 4: 3} if groups >= 4 else {0: 1, 1: 2, 2: 3}
+    for slot, (src, own) in enumerate(slots):
+        if not own:
+            arrived(src)
+        prepare(slot, src)
+    places = {1: 1, 2: 2, 3: 3, 7: 4} if groups >= 4 else {0: 1, 1: 2, 2: 3, 3: 4}
     acc_k, acc_v = s_buf.at[1, 0:group, 0:128], s_buf.at[1, 0:group, 128:256]
     halves = chunks % 4 == 0
 
@@ -519,33 +525,40 @@
 
     def send_q(side):
         def turn(j, _):
-            c = lax.rem(first_chunk + j, chunks)
+            c = j
             x = dqt[:, rows_at(c, BLK)] * (HD**-0.5)
             aux[rows_at(c, BLK), :] = jnp.concatenate([x, jnp.zeros_like(x)], axis=0).T
             return 0
 
         lax.fori_loop(side * chunks // 2, (side + 1) * chunks // 2, turn, 0)
 
-        def send(d, _):
-            owner = lax.rem(first_group * owners + d, n)
-            top = aux[rows_at(2 * owner, half), :]
-            bottom = aux[rows_at(2 * owner + 1, half), :]
+        for slot in range(side * n // 2, (side + 1) * n // 2):
+            owner, own = slots[slot]
+            top = aux[slot * rows : slot * rows + half, :]
+            bottom = aux[slot * rows + half : (slot + 1) * rows, :]
             q_send[owner] = jnp.where(low_lanes(half), top, swap(bottom)).astype(BF)
-
-            @pl.when(owner != me)
-            def _():
+            if own:
+                q_recv[owner] = q_send[owner]
+            else:
                 q_copy(owner, me, owner).start()
 
-            @pl.when(owner == me)
-            def _():
-                q_recv[owner] = q_send[owner]
-
-            return 0
-
-        lax.fori_loop(side * n // 2, (side + 1) * n // 2, send, 0)
+    def send_kv(g):
+        for w in range(owners):
+            owner, own = slots[g * owners + w]
+            cut = slice(w * rows, (w + 1) * rows)
+            kv_send[owner] = jnp.where(low_lanes(rows), acc_k[cut, :], acc_v[cut, :]).astype(BF)
+            if own:
+                kv_recv[owner] = kv_send[owner]
+            else:
+                kv_copy(owner, me, owner).start()
+
+    def hooks(i, h):
+        for place, number in places.items():
+            if place % 2 == h:
+                pl.when(i == place // 2)(steps[number])
 
     def one_group(i, _):
-        g = lax.rem(first_group + i, groups)
+        g = i
         acc_k[...] = jnp.zeros_like(acc_k)
         acc_v[...] = jnp.zeros_like(acc_v)
 
@@ -553,11 +566,11 @@
             return dot(vx[rows_at(g * SUB + r, BLK), :], of[rows_at(c, BLK), :], 1, 1)
 
         for r in range(SUB):
-            s_buf[0, r * BLK : (r + 1) * BLK, :] = prob_back(r, first_chunk)
+            s_buf[0, r * BLK : (r + 1) * BLK, :] = prob_back(r, 0)
 
         def two_chunks(pair, _):
             for par in range(2):
-                c = lax.rem(2 * pair + par + first_chunk, chunks)
+                c = 2 * pair + par
                 ahead = lax.rem(c + 1, chunks)
                 q_d = qd[rows_at(c, BLK), :]
                 dq = jnp.zeros((HD, BLK), F32)
@@ -577,29 +590,22 @@
 
         for h in range(2):
             lax.fori_loop(h * chunks // 4, (h + 1) * chunks // 4, two_chunks, 0)
-            for place, number in places.items():
-                if place % 2 == h:
-                    pl.when(i == place // 2)(steps[number])
-            if h == 0 and halves:
-                pl.when(i == groups - 1)(functools.partial(send_q, 0))
-        for w in range(owners):
-            owner = g * owners + w
-            cut = slice(w * rows, (w + 1) * rows)
-            kv_send[owner] = jnp.where(low_lanes(rows), acc_k[cut, :], acc_v[cut, :]).astype(BF)
-
-            @pl.when(owner != me)
-            def _():
-                kv_copy(owner, me, owner).start()
-
-            @pl.when(owner == me)
-            def _():
-                kv_recv[owner] = kv_send[owner]
-
+            if h == 0:
+                hooks(i, h)
+                if halves:
+                    pl.when(i == groups - 1)(functools.partial(send_q, 0))
+        for group_at in range(groups):
+            pl.when(i == group_at)(functools.partial(send_kv, group_at))
+        hooks(i, 1)
         return 0
 
     lax.fori_loop(0, groups, one_group, 0)
     for side in range(1 if halves else 0, 2):
         send_q(side)
+
+    steps[5]()
+    copies[0].start()
+    copies[1].start()
 
     def settle_kv(d, _):
         peer = lax.rem(me + d, n)
@@ -608,7 +614,7 @@
         return 0
 
     lax.fori_loop(1, n, settle_kv, 0)
-    steps[4]()
+    copies[2].start()
 
     def settle_q(d, _):
         peer = lax.rem(me + d, n)
@@ -617,14 +623,14 @@
         return 0
 
     lax.fori_loop(1, n, settle_q, 0)
-    steps[5]()
+    copies[3].start()
 
 
 def layer_kernel(
-    starts, q_ref, k_ref, v_ref, w_hbm, cot_hbm, taps_hbm,
-    layer_out, kv_recv, q_recv, w_out, conv_out,
-    w_ref, cot_ref, taps_ref, mixed, sums, conv_sums,
-    kx, qx, vx, kt, s_buf, p_buf, aux, back_recv, in_sem, *rest,
+    starts, q_hbm, k_hbm, v_hbm, w_hbm, cot_hbm, taps_hbm,
+    layer_hbm, kv_hbm, qg_hbm, w_out_hbm, conv_hbm,
+    q_ref, k_ref, v_ref, w_ref, cot_ref, taps_ref, layer_out, kv_recv, q_recv, w_out, conv_out,
+    mixed, sums, conv_sums, kx, qx, vx, kt, s_buf, p_buf, aux, back_recv, in_sem, out_sem, *rest,
 ):
     rest = list(rest)
 
@@ -633,34 +639,44 @@
         del rest[:count]
         return taken
 
+    greeted = greet(("seq", "dp"))
+    sources = (q_hbm, k_hbm, v_hbm, w_hbm, cot_hbm, taps_hbm)
+    places = (q_ref, k_ref, v_ref, w_ref, cot_ref, taps_ref)
     loads = [
-        pltpu.make_async_copy(w_hbm, w_ref, in_sem.at[0]),
-        pltpu.make_async_copy(cot_hbm, cot_ref, in_sem.at[1]),
-        pltpu.make_async_copy(taps_hbm, taps_ref, in_sem.at[2]),
+        pltpu.make_async_copy(source, place, in_sem.at[i])
+        for i, (source, place) in enumerate(zip(sources, places))
     ]
     for load in loads:
         load.start()
+    results = ((w_out, w_out_hbm), (conv_out, conv_hbm), (kv_recv, kv_hbm), (q_recv, qg_hbm), (layer_out, layer_hbm))
+    copies = [
+        pltpu.make_async_copy(source, place, out_sem.at[i]) for i, (source, place) in enumerate(results)
+    ]
     qk_send, v_send, qk_recv, v_recv, vt, mix_send, mix_recv = take(7)
     attend(
-        starts, q_ref, k_ref, v_ref, mixed,
+        starts, q_ref, k_ref, v_ref, loads, greeted, mixed,
         qk_send, v_send, qk_recv, v_recv, kx, qx, vx, kt, vt, s_buf, p_buf, aux, mix_send, mix_recv,
         *take(6),
     )
-    for load in loads:
+    for load in loads[3:]:
         load.wait()
     bufs = take(12)
     sems = take(8)
     reduce_bufs = take(8)
     steps = reducer(sums, conv_sums, w_out, conv_out, reduce_bufs, take(10))
-    convolve(
+    arrived, settle_back = convolve(
         starts, mixed, w_ref, cot_ref, taps_ref, layer_out, sums, conv_sums, steps[0],
         *bufs, back_recv, *sems,
     )
+    copies[4].start()
     of, qd, dqt, kv_send, q_send = take(5)
     attend_back(
-        p_buf, vx, qx, kt, aux, back_recv, kv_recv, q_recv, steps,
+        p_buf, vx, qx, kt, aux, back_recv, arrived, kv_recv, q_recv, copies, steps,
         of, qd, s_buf, dqt, kv_send, q_send, *rest,
     )
+    settle_back()
+    for copy in copies:
+        copy.wait()
 
 
 def layer(starts, q, k, v, weight, cot, taps):
@@ -669,7 +685,10 @@
     total, half = n * rows, rows // 2
     shape, vmem, dma = jax.ShapeDtypeStruct, pltpu.VMEM, pltpu.SemaphoreType.DMA
     bufs, sems = reducer_bufs(width, n, groups)
-    wide, narrow = vmem((n, rows, 128), BF), vmem((n, half, 128), BF)
+    wide, narrow, square = vmem((n, rows, 128), BF), vmem((n, half, 128), BF), vmem((width, width), BF)
+    frames, lanes = vmem((rows, width), BF), vmem((total, 128), BF)
+    taps_all, taps_half = vmem((KERN + 1, width), F32), vmem(((KERN + 1) // 2, width), F32)
+    padded = vmem((2, rows + HALO, width), F32)
     per_peer = dma((n,))
     return pl.pallas_call(
         layer_kernel,
@@ -680,26 +699,24 @@
             shape((width, width), BF),
             shape((KERN + 1, width), F32),
         ],
-        in_specs=[SM, VM, VM, VM, ANY, ANY, ANY],
-        out_specs=[VM] * 5,
+        in_specs=[SM] + [ANY] * 6,
+        out_specs=[ANY] * 5,
         scratch_shapes=[
-            vmem((width, width), BF), vmem((rows, width), BF), vmem((KERN, width), F32),
-            vmem((rows, width), BF),
-            vmem((width // 2, width), BF), vmem(((KERN + 1) // 2, width), F32),
-            vmem((total, 128), BF), vmem((total, 128), BF), vmem((total, 128), BF),
-            vmem((HD, total), BF),
+            frames, frames, frames, square, frames, vmem((KERN, width), F32),
+            frames, wide, narrow, square, taps_all,
+            frames, vmem((width // 2, width), BF), taps_half,
+            lanes, lanes, lanes, vmem((HD, total), BF),
             vmem((SUB, total, BLK), F32), vmem((total // BLK, total, BLK), BF),
-            vmem((total, 128), F32), narrow, dma((3,)),
+            vmem((total, 128), F32), narrow, dma((6,)), dma((5,)),
             wide, narrow, wide, narrow, vmem((HD + 16, total), BF), narrow, narrow,
             *[per_peer] * 6,
-            vmem((width, width), BF), vmem((KERN + 1, width), F32),
-            vmem((width // 2, width), BF), vmem(((KERN + 1) // 2, width), F32),
-            vmem((rows, width), BF), vmem((HALO, width), BF), vmem((2, rows + HALO, width), F32),
-            vmem((rows, width), F32), vmem((HALO, width), BF), vmem((2, rows + HALO, width), F32),
-            vmem((rows, width), BF), narrow,
+            square, taps_all, vmem((width // 2, width), BF), taps_half,
+            frames, vmem((HALO, width), BF), padded,
+            vmem((rows, width), F32), vmem((HALO, width), BF), padded,
+            frames, narrow,
             dma, dma, dma, dma, per_peer, per_peer, dma((2,)), dma((2,)),
             *bufs, *sems,
-            vmem((total, 128), BF), vmem((total, 128), BF), vmem((HD, total), F32), wide, narrow,
+            lanes, lanes, vmem((HD, total), F32), wide, narrow,
             *[per_peer] * 4,
         ],
         compiler_params=pltpu.CompilerParams(
@@ -715,12 +732,14 @@
     rows = kv_ref.shape[1]
     half = rows // 2
     low = low_lanes(rows)
-    one, two = kv_ref[0].astype(F32), kv_ref[1].astype(F32)
-    dk_out[...] = jnp.where(low, one, swap(two)).astype(BF)
-    dv_out[...] = jnp.where(low, swap(one), two).astype(BF)
-    top, bottom = unpack_halves(q_ref[0].astype(F32), q_ref[1].astype(F32))
-    dq_out[0:half, :] = top.astype(BF)
-    dq_out[half:rows, :] = bottom.astype(BF)
+    for t in range(kv_ref.shape[0] // 2):
+        cut = slice(t * 128, (t + 1) * 128)
+        one, two = kv_ref[2 * t].astype(F32), kv_ref[2 * t + 1].astype(F32)
+        dk_out[:, cut] = jnp.where(low, one, swap(two)).astype(BF)
+        dv_out[:, cut] = jnp.where(low, swap(one), two).astype(BF)
+        top, bottom = unpack_halves(q_ref[2 * t].astype(F32), q_ref[2 * t + 1].astype(F32))
+        dq_out[0:half, cut] = top.astype(BF)
+        dq_out[half:rows, cut] = bottom.astype(BF)
     layer_out[...] = layer_ref[...]
     w_out[...] = w_ref[...].astype(F32) * factor
     conv_out[...] = conv_ref[0:KERN, :] * factor
@@ -728,23 +747,24 @@
 
 def finish(kv, q, layer, w_sum, conv_sum, factor):
     rows, width = layer.shape
-    steps = width // 128
+    steps = STEPS
+    wide, heads = width // steps, width // HD // steps
     shape = jax.ShapeDtypeStruct
-    column = pl.BlockSpec((rows, 128), lambda t: (0, t))
-    band = pl.BlockSpec((width // steps, width), lambda t: (t, 0))
+    column = pl.BlockSpec((rows, wide), lambda t: (0, t))
+    band = pl.BlockSpec((wide, width), lambda t: (t, 0))
     return pl.pallas_call(
         functools.partial(finish_kernel, factor),
         grid=(steps,),
         out_shape=[shape((rows, width), BF)] * 4
         + [shape((width, width), F32), shape((KERN, width), F32)],
         in_specs=[
-            pl.BlockSpec((2, rows, 128), lambda t: (t, 0, 0)),
-            pl.BlockSpec((2, rows // 2, 128), lambda t: (t, 0, 0)),
+            pl.BlockSpec((heads, rows, 128), lambda t: (t, 0, 0)),
+            pl.BlockSpec((heads, rows // 2, 128), lambda t: (t, 0, 0)),
             column,
             band,
-            pl.BlockSpec((KERN + 1, 128), lambda t: (0, t)),
+            pl.BlockSpec((KERN + 1, wide), lambda t: (0, t)),
         ],
-        out_specs=[column] * 4 + [band, pl.BlockSpec((KERN, 128), lambda t: (0, t))],
+        out_specs=[column] * 4 + [band, pl.BlockSpec((KERN, wide), lambda t: (0, t))],
         name="finish",
     )(kv, q, layer, w_sum, conv_sum)
 

time: 147 us -> 133 us (0.905)
  Pallas kernels: 146 us -> 132 us
    pallas_call x1, Pallas kernels: 139 us -> 128 us  [layer(): pl.pallas_call(layer_kernel, out_shape=[shape((rows, width), BF), shape((...]
    pallas_call x1, Pallas kernels: 6.82 us -> 4.24 us  [finish(): pl.pallas_call(functools.partial(finish_kernel, factor), grid=(steps,), o...]
where the time goes in v4:
time: 133 us; the launch traced here: 132 us
  Pallas kernels  132 us (99%)
    pallas_call x1, Pallas kernels, layer(): pl.pallas_call(layer_kernel, out_shape=[shape((rows, width), BF), shape((...  128 us
    pallas_call x1, Pallas kernels, finish(): pl.pallas_call(functools.partial(finish_kernel, factor), grid=(steps,), o...  4.24 us

profile of v4, /device:TPU:1, one launch (start us, length us, event | category | flops | bytes accessed | tf_op | source)
XLA Modules:
  0.0 132.4 jit_solution(4246552008986078027)
XLA Ops:
  0.6 127.6 %layer.1 = (bf16[192,1024]{1,0:T(8,128)(2,1)}, bf16[16,192,128]{2,1,0:T(8,128)(2,1)}, bf16[16,96,128]{2,1,0:T(8,128)(2,1)}, bf16[1024,1024]{1,0:T(8,128)(2,1)}, f32[32,1024]{1,0:T(8,128)}) custom-call(s32[1,2]{1,0:T(1,128)} %starts.1, bf16[192,1024]{1,0:T(8,128)(2,1)} %bitcast.8, bf16[192,1024]{1,0:T(8,128)(2,1)} %bitcast.9, bf16[192,1024]{1,0:T(8,128)(2,1)} %bitcast.10, ...), custom_call_target="tpu_custom_call" | custom-call | tf_op jit(solution)/shard_map/layer/pallas_call | solution.py:693
  128.2 4.2 %finish.1 = (bf16[192,1024]{1,0:T(8,128)(2,1)}, bf16[192,1024]{1,0:T(8,128)(2,1)}, bf16[192,1024]{1,0:T(8,128)(2,1)}, bf16[192,1024]{1,0:T(8,128)(2,1)}, f32[1024,1024]{1,0:T(8,128)}, /*index=5*/f32[31,1024]{1,0:T(8,128)}) custom-call(bf16[16,192,128]{2,1,0:T(8,128)(2,1)} %get-tuple-element.17.kv_ref, bf16[16,96,128]{2,1,0:T(8,128)(2,1)} %get-tuple-element.18.q_ref, ...), custom_call_target="tpu_custom_call" | custom-call | tf_op jit(solution)/shard_map/finish/pallas_call | solution.py:755

commit v5 on v4

--- a/solution.py
+++ b/solution.py
@@ -501,7 +501,7 @@
         if not own:
             arrived(src)
         prepare(slot, src)
-    places = {1: 1, 2: 2, 3: 3, 7: 4} if groups >= 4 else {0: 1, 1: 2, 2: 3, 3: 4}
+    places = {2: 1, 4: 2, 5: 3} if groups >= 4 else {0: 1, 1: 2, 2: 3}
     acc_k, acc_v = s_buf.at[1, 0:group, 0:128], s_buf.at[1, 0:group, 128:256]
     halves = chunks % 4 == 0
 
@@ -603,9 +603,7 @@
     for side in range(1 if halves else 0, 2):
         send_q(side)
 
-    steps[5]()
-    copies[0].start()
-    copies[1].start()
+    steps[4]()
 
     def settle_kv(d, _):
         peer = lax.rem(me + d, n)
@@ -624,6 +622,9 @@
 
     lax.fori_loop(1, n, settle_q, 0)
     copies[3].start()
+    steps[5]()
+    copies[0].start()
+    copies[1].start()
 
 
 def layer_kernel(

time: 133 us -> 128 us (0.962)
  Pallas kernels: 132 us -> 128 us
    pallas_call x1, Pallas kernels: 128 us -> 123 us  [layer(): pl.pallas_call(layer_kernel, out_shape=[shape((rows, width), BF), shape((...]
where the time goes in v5:
time: 128 us
  Pallas kernels  128 us (100%)
    pallas_call x1, Pallas kernels, layer(): pl.pallas_call(layer_kernel, out_shape=[shape((rows, width), BF), shape((...  123 us
    pallas_call x1, Pallas kernels, finish(): pl.pallas_call(functools.partial(finish_kernel, factor), grid=(steps,), o...  4.24 us

profile of v5, /device:TPU:1, one launch (start us, length us, event | category | flops | bytes accessed | tf_op | source)
XLA Modules:
  0.0 128.3 jit_solution(17556057364374084569)
XLA Ops:
  0.6 123.4 %layer.1 = (bf16[192,1024]{1,0:T(8,128)(2,1)}, bf16[16,192,128]{2,1,0:T(8,128)(2,1)}, bf16[16,96,128]{2,1,0:T(8,128)(2,1)}, bf16[1024,1024]{1,0:T(8,128)(2,1)}, f32[32,1024]{1,0:T(8,128)}) custom-call(s32[1,2]{1,0:T(1,128)} %starts.1, bf16[192,1024]{1,0:T(8,128)(2,1)} %bitcast.8, bf16[192,1024]{1,0:T(8,128)(2,1)} %bitcast.9, bf16[192,1024]{1,0:T(8,128)(2,1)} %bitcast.10, ...), custom_call_target="tpu_custom_call" | custom-call | tf_op jit(solution)/shard_map/layer/pallas_call | solution.py:694
  124.0 4.2 %finish.1 = (bf16[192,1024]{1,0:T(8,128)(2,1)}, bf16[192,1024]{1,0:T(8,128)(2,1)}, bf16[192,1024]{1,0:T(8,128)(2,1)}, bf16[192,1024]{1,0:T(8,128)(2,1)}, f32[1024,1024]{1,0:T(8,128)}, /*index=5*/f32[31,1024]{1,0:T(8,128)}) custom-call(bf16[16,192,128]{2,1,0:T(8,128)(2,1)} %get-tuple-element.17.kv_ref, bf16[16,96,128]{2,1,0:T(8,128)(2,1)} %get-tuple-element.18.q_ref, ...), custom_call_target="tpu_custom_call" | custom-call | tf_op jit(solution)/shard_map/finish/pallas_call | solution.py:756
